TPU v7x, 32 devices: a whole 2x2x4 slice. The times are simulated.
32 devices in a mesh: seq: 8 (over z, y), tp: 4 (over x, core).
Axes of the slice: x: 2, y: 2, z: 4, core: 2. Of those that a mesh axis runs over, the one named last changes fastest.
Arguments:
- x_in: bfloat16 [1024, 8192], P('seq', 'tp'), may hold values from -6 to 6
- gate_in: bfloat16 [1024, 8192], P('seq', 'tp'), may hold values from -6 to 6
- conv_weight: float32 [4, 8192], P(None, 'tp'), may hold values from -3 to 3
- conv_bias: float32 [8192], P('tp'), may hold values from -0.5 to 0.5
- x_weight: bfloat16 [8192, 544], P('tp'), may hold values from -0.0625 to 0.0625
- dt_weight: bfloat16 [512, 8192], P(None, 'tp'), may hold values from -0.25 to 0.25
- dt_bias: float32 [8192], P('tp'), may hold values from -5 to -2.5
- decay_rate: float32 [8192, 16], P('tp'), may hold values from 0 to 4
- skip_gain: float32 [8192], P('tp'), may hold values from 0.5 to 1.5
- out_weight: bfloat16 [8192, 4096], P('tp'), may hold values from -0.0625 to 0.0625
- residual_in: bfloat16 [1024, 4096], P(('seq', 'tp')), may hold values from -36 to 36
- norm_gain: float32 [4096], replicated, may hold values from 0.1 to 1.9
- expert_ids: int32 [1024, 2], P(('seq', 'tp')), may hold values from 0 to 7, all different within a row; in each aligned block of 32 rows (0 to 31, 32 to 63, ...) at most 12 rows name the same one
- gate_prob: float32 [1024, 2], P(('seq', 'tp')), may hold values from 0.1 to 1
- up_weight: bfloat16 [4096, 98304], P(None, ('seq', 'tp')), may hold values from -0.09375 to 0.09375
- down_weight: bfloat16 [98304, 4096], P(('seq', 'tp')), may hold values from -0.0546875 to 0.0546875
Outputs:
- mixer_out: bfloat16 [1024, 4096], P(('seq', 'tp'))
- layer_out: bfloat16 [1024, 4096], P(('seq', 'tp'))
Inputs may be any that keep to these rules, and one draw needn't show every extreme that they name: `expert_ids`: each row names two different experts. In each device's aligned block of 32 rows no expert is named by more than 12 rows, a bound that some block reaches.
All inputs are finite; a program needn't handle non-finite values.
Results may differ from a plain program's by a relative error of at most 0.007.
Values may be sent and summed in bfloat16 or wider, within the bound.
A program may use at most 192 MiB of HBM per device.

v0:
```python
import jax
import jax.numpy as jnp
from jax import lax
from jax.sharding import PartitionSpec as P

STATE = 16
DTRANK = 512
EXPERTS = 8


def shifted(value, axis, steps):
    count = lax.axis_size(axis)
    initial, last = (max(0, -steps), min(count, count - steps))
    return lax.ppermute(value, axis, [(source, source + steps) for source in range(initial, last)])


def prefix(part, axis, combine, identity):
    place = lax.axis_index(axis)
    gathered = jax.tree.map(lambda a: lax.all_gather(a, axis), part)
    state = jax.tree.map(lambda a, e: jnp.zeros_like(a) + jnp.asarray(e, a.dtype), part, identity)

    def one(hop, state):
        return combine(
            state, jax.tree.map(lambda a: lax.dynamic_index_in_dim(a, hop, 0, False), gathered)
        )

    return lax.fori_loop(0, place, one, state)


def chain_join(earlier, later):
    return (earlier[0] * later[0], later[0] * earlier[1] + later[1])


def recur_blocks(start_state, step_cols, drive_cols, entry_cols, readout_cols, negative_rate):

    def advance(carried, columns):
        step_row, drive_row, entry_row, readout_row = columns
        carried = (
            jnp.exp(step_row[:, None, :] * negative_rate[None]) * carried
            + entry_row[:, :, None] * drive_row[:, None, :]
        )
        return (carried, jnp.sum(readout_row[:, :, None] * carried, axis=1))

    return lax.scan(advance, start_state, (step_cols, drive_cols, entry_cols, readout_cols))


def by_position(values, blocks, span):
    return values.reshape(blocks, span, values.shape[1]).transpose(1, 0, 2)


def expert_share(arrived_flat, up_weight, down_weight):
    hidden = jax.nn.silu(
        jnp.dot(arrived_flat, up_weight, preferred_element_type=jnp.float32)
    ).astype(jnp.bfloat16)
    return jnp.dot(hidden, down_weight, preferred_element_type=jnp.float32).astype(jnp.bfloat16)


def per_device(
    x_in,
    gate_in,
    conv_weight,
    conv_bias,
    x_weight,
    dt_weight,
    dt_bias,
    decay_rate,
    skip_gain,
    out_weight,
    residual_in,
    norm_gain,
    expert_ids,
    gate_prob,
    up_weight,
    down_weight,
):
    tokens, channels = x_in.shape
    width = out_weight.shape[1]
    reach = conv_weight.shape[0] - 1
    rim_rows = shifted(x_in[tokens - reach :], "seq", 1)
    padded = jnp.concatenate([rim_rows, x_in], axis=0).astype(jnp.float32)
    conv_out = conv_bias[None, :] + sum(
        (
            conv_weight[offset][None, :] * padded[offset : offset + tokens]
            for offset in range(reach + 1)
        )
    )
    inner = jax.nn.silu(conv_out).astype(jnp.bfloat16)
    projected = lax.psum(jnp.dot(inner, x_weight, preferred_element_type=jnp.float32), "tp")
    dt_low = projected[:, :DTRANK].astype(jnp.bfloat16)
    entry_rows = projected[:, DTRANK : DTRANK + STATE]
    readout_rows = projected[:, DTRANK + STATE :]
    step_size = jax.nn.softplus(
        jnp.dot(dt_low, dt_weight, preferred_element_type=jnp.float32) + dt_bias[None, :]
    )
    drive = step_size * inner.astype(jnp.float32)
    negative_rate = -decay_rate.T
    span = 16
    blocks = tokens // span
    step_cols = by_position(step_size, blocks, span)
    drive_cols = by_position(drive, blocks, span)
    entry_cols = by_position(entry_rows, blocks, span)
    readout_cols = by_position(readout_rows, blocks, span)
    zero_blocks = jnp.zeros((blocks, STATE, channels), jnp.float32)
    block_ends, local_out = recur_blocks(
        zero_blocks, step_cols, drive_cols, entry_cols, readout_cols, negative_rate
    )
    block_decay = jnp.exp(negative_rate[None] * jnp.sum(step_cols, axis=0)[:, None, :])
    decay_through, state_through = lax.associative_scan(
        chain_join, (block_decay, block_ends), axis=0
    )
    ones_state = jnp.ones((STATE, channels), jnp.float32)
    zeros_state = jnp.zeros((STATE, channels), jnp.float32)
    entering = prefix(
        (decay_through[-1], state_through[-1]), "seq", chain_join, (ones_state, zeros_state)
    )[1]
    decay_before = jnp.concatenate([ones_state[None], decay_through[:-1]], axis=0)
    state_before = jnp.concatenate([zeros_state[None], state_through[:-1]], axis=0)
    block_starts = decay_before * entering[None] + state_before
    ssm_cols = recur_blocks(
        block_starts, step_cols, drive_cols, entry_cols, readout_cols, negative_rate
    )[1]
    ssm = ssm_cols.transpose(1, 0, 2).reshape(tokens, channels)
    mixed = (
        (ssm + skip_gain[None, :] * inner.astype(jnp.float32))
        * jax.nn.silu(gate_in.astype(jnp.float32))
    ).astype(jnp.bfloat16)
    rows = tokens // lax.axis_size("tp")
    mixer_sum = lax.psum_scatter(
        jnp.dot(mixed, out_weight, preferred_element_type=jnp.float32),
        "tp",
        scatter_dimension=0,
        tiled=True,
    )
    mixer_out = (mixer_sum + residual_in.astype(jnp.float32)).astype(jnp.bfloat16)
    mixer_wide = mixer_out.astype(jnp.float32)
    normed = (
        mixer_wide
        * lax.rsqrt(jnp.mean(mixer_wide * mixer_wide, axis=1, keepdims=True) + 1e-06)
        * norm_gain[None, :]
    ).astype(jnp.bfloat16)
    seq_count = lax.axis_size("seq")
    devices = seq_count * lax.axis_size("tp")
    seq_group = seq_count // EXPERTS
    capacity = 3 * rows // EXPERTS
    chosen = expert_ids.reshape(-1)
    expert_hits = (chosen[:, None] == jnp.arange(EXPERTS, dtype=jnp.int32)[None, :]).astype(
        jnp.int32
    )
    earlier_hits = jnp.cumsum(expert_hits, axis=0) - expert_hits
    slot_index = jnp.sum(earlier_hits * expert_hits, axis=1)
    target = chosen * capacity + slot_index
    placing = (jnp.arange(EXPERTS * capacity, dtype=jnp.int32)[:, None] == target[None, :]).astype(
        jnp.bfloat16
    )
    placing = jnp.sum(placing.reshape(EXPERTS * capacity, rows, 2), axis=2)
    slots_out = (
        jnp.dot(placing, normed, preferred_element_type=jnp.float32)
        .astype(jnp.bfloat16)
        .reshape(EXPERTS, capacity, width)
    )
    along_seq = jnp.repeat(slots_out, seq_group, axis=0)
    arrived_seq = lax.all_to_all(along_seq, "seq", split_axis=0, concat_axis=0, tiled=True)
    arrived_all = lax.all_gather(
        arrived_seq.reshape(1, seq_count * capacity, width), "tp", axis=0, tiled=True
    )
    arrived_flat = arrived_all.reshape(devices * capacity, width)
    summed = lax.psum_scatter(
        expert_share(arrived_flat, up_weight, down_weight).astype(jnp.float32).astype(jnp.bfloat16),
        "tp",
        scatter_dimension=0,
        tiled=True,
    ).astype(jnp.float32)
    home = lax.all_to_all(
        summed.reshape(seq_count, capacity, width).astype(jnp.bfloat16),
        "seq",
        split_axis=0,
        concat_axis=0,
        tiled=True,
    ).astype(jnp.float32)
    expert_out = jnp.sum(home.reshape(EXPERTS, seq_group, capacity, width), axis=1).reshape(
        EXPERTS * capacity, width
    )
    picked = jnp.take(expert_out, target, axis=0).reshape(rows, 2, width)
    layer_out = (mixer_wide + jnp.sum(picked * gate_prob[:, :, None], axis=1)).astype(jnp.bfloat16)
    return (mixer_out, layer_out)


def solution(mesh):
    return jax.shard_map(
        per_device,
        mesh=mesh,
        in_specs=(
            P("seq", "tp"),
            P("seq", "tp"),
            P(None, "tp"),
            P("tp"),
            P("tp", None),
            P(None, "tp"),
            P("tp"),
            P("tp", None),
            P("tp"),
            P("tp", None),
            P(("seq", "tp"), None),
            P(),
            P(("seq", "tp"), None),
            P(("seq", "tp"), None),
            P(None, ("seq", "tp")),
            P(("seq", "tp"), None),
        ),
        out_specs=(P(("seq", "tp"), None), P(("seq", "tp"), None)),
        check_vma=False,
    )
```

profile of v0, /device:TPU:13, one launch (start us, length us, event | category | flops | bytes accessed | tf_op | source)
XLA Modules:
  0.0 460.6 jit_solution(15491746981362353329)
XLA Ops:
  8.1 3.1 collective-permute-start
  13.8 1.4 multiply_convert_fusion.2
  16.1 1.5 fusion.39
  17.7 33.4 %all-reduce.16.cloned.1.call-done = f32[128,544]{0,1:T(8,128)} async-done(((f32[128,544]{0,1:T(8,128)}), f32[128,544]{0,1:T(8,128)}) %all-reduce.16.cloned.1.call-update) | async-done | bytes 278544 | tf_op jit(solution)/shard_map/psum | solution.py:88
  51.1 2.7 convert_multiply_fusion.2
  54.4 2.6 copy_bitcast_fusion
  57.0 1.3 fusion.34
  58.5 22.9 %while.37 = (s32[]{:T(128)}, f32[8,16,2048]{2,1,0:T(8,128)S(1)}, f32[16,8,2048]{2,1,0:T(8,128)}, f32[16,2048]{1,0:T(8,128)S(1)}, f32[16,8,16]{2,1,0:T(8,128)S(1)...) while((s32[]{:T(128)}, f32[8,16,2048]{2,1,0:T(8,128)S(1)}, f32[16,8,2048]{2,1,0:T(8,128)}, ...), condition=%wide.region_3.4_spmd.clone, body=%wide.region_2.3_spmd.clone.sunk | while | flops 1310723 | bytes 2623079 | solution.py:44
  85.3 2.4 pad.48
  87.7 2.4 pad.49
  90.1 2.1 add.214
  92.2 4.2 pad.102
  96.3 1.6 pad_maximum_fusion.2
  98.0 2.4 pad.42
  100.4 2.4 pad.43
  102.9 2.2 add_multiply_fusion.1
  105.1 2.4 pad.50
  107.5 1.6 slice_add_fusion.3
  109.2 1.3 add.207
  110.5 2.3 pad.104
  112.8 1.6 slice.276
  114.5 2.3 pad.45
  116.8 2.4 pad.67
  119.2 1.9 pad_maximum_fusion
  121.2 4.2 pad.44
  126.3 2.4 slice_add_fusion.5
  129.7 18.2 %all-gather.6.cloned.1.call-done = f32[8,16,2048]{2,1,0:T(8,128)} async-done(((f32[1,16,2048]{2,1,0:T(8,128)}), f32[8,16,2048]{2,1,0:T(8,128)}) %all-gather.6.cloned.1.call-update) | async-done | bytes 1048592 | tf_op jit(solution)/shard_map/all_gather | solution.py:19
  147.9 41.6 %all-gather.4.cloned.1.call-done = f32[8,16,2048]{2,1,0:T(8,128)} async-done(((f32[1,16,2048]{2,1,0:T(8,128)}), f32[8,16,2048]{2,1,0:T(8,128)}) %all-gather.4.cloned.1.call-update) | async-done | bytes 1048592 | tf_op jit(solution)/shard_map/all_gather | solution.py:19
  189.6 3.4 while.35
  193.0 1.3 pad_add_fusion
  194.3 36.9 %while.36 = (s32[]{:T(128)}, f32[8,16,2048]{2,1,0:T(8,128)S(1)}, f32[16,8,2048]{2,1,0:T(8,128)}, f32[16,8,2048]{2,1,0:T(8,128)}, f32[16,2048]{1,0:T(8,128)S(1)},...) while((s32[]{:T(128)}, f32[8,16,2048]{2,1,0:T(8,128)S(1)}, ...), condition=%wide.region_8.9_spmd, body=%wide.region_6.8_spmd.sunk | while | flops 1556482 | bytes 2821733 | solution.py:44
  231.3 1.8 copy.55
  234.2 9.5 %fusion.40 = f32[128,4096]{1,0:T(8,128)} fusion(bf16[128,2048]{1,0:T(8,128)(2,1)S(1)} %fusion.4, bf16[2048,4096]{1,0:T(8,128)(2,1)} %param.31), kind=kOutput, calls=%fused_computation.108 | convolution fusion | flops 2147483648 | bytes 19398656 | tf_op jit(solution)/shard_map/dot_general | solution.py:129
  244.6 36.2 %reduce-scatter.3.cloned.1.call-done = f32[32,4096]{1,0:T(8,128)} async-done(((f32[128,4096]{1,0:T(8,128)}), f32[32,4096]{1,0:T(8,128)}) %reduce-scatter.3.cloned.1.call-update) | async-done | bytes 524304 | tf_op jit(solution)/shard_map/reduce_scatter | solution.py:128
  280.8 1.2 fusion.12
  283.4 28.0 %all_to_all.10 = bf16[8,12,4096]{2,1,0:T(8,128)(2,1)S(1)} all-to-all(bf16[8,12,4096]{2,1,0:T(8,128)(2,1)S(1)} %reshape_broadcast_in_dim_reshape.3), channel_id=1, replica_groups=mesh['seq'=8,'tp'=4] {'seq'}, dimensions={0} | all-to-all | bytes 1572864 | tf_op jit(solution)/shard_map/all_to_all | solution.py:162
  312.8 30.0 %all-gather.8.cloned.1.call-done = bf16[4,96,4096]{2,1,0:T(8,128)(2,1)} async-done(((bf16[1,96,4096]{2,1,0:T(8,128)(2,1)}), bf16[4,96,4096]{2,1,0:T(8,128)(2,1)}) %all-gather.8.cloned.1.call-update) | async-done | bytes 3145744 | tf_op jit(solution)/shard_map/all_gather | solution.py:163
  342.8 16.0 %multiply_convert_fusion.5 = bf16[384,3072]{1,0:T(8,128)(2,1)S(1)} fusion(bf16[384,4096]{1,0:T(8,128)(2,1)} %bitcast.97, bf16[4096,3072]{1,0:T(8,128)(2,1)} %param.36), kind=kOutput, calls=%fused_computation.16.clone.clone.1 | convolution fusion | flops 9669574656 | bytes 30670848 | tf_op jit(solution)/shard_map/dot_general | solution.py:53
  358.8 15.9 %convolution_convert_fusion = bf16[384,4096]{1,0:T(8,128)(2,1)} fusion(bf16[3072,4096]{1,0:T(8,128)(2,1)} %param.37, bf16[384,3072]{1,0:T(8,128)(2,1)S(1)} %multiply_convert_fusion.5), kind=kOutput, calls=%fused_computation.15 | convolution fusion | flops 9665249280 | bytes 30670848 | tf_op jit(solution)/shard_map/dot_general | solution.py:55
  374.7 37.7 %reduce-scatter.5.cloned.1.call-done = bf16[96,4096]{1,0:T(8,128)(2,1)} async-done(((bf16[384,4096]{1,0:T(8,128)(2,1)}), bf16[96,4096]{1,0:T(8,128)(2,1)}) %reduce-scatter.5.cloned.1.call-update) | async-done | bytes 786448 | tf_op jit(solution)/shard_map/reduce_scatter | solution.py:167
  412.4 2.2 convert_element_type.72
  414.6 5.5 %all-to-all-start.1 = ((bf16[8,12,4096]{2,1,0:T(8,128)(2,1)}), bf16[8,12,4096]{2,1,0:T(8,128)(2,1)S(1)}, u32[]{:S(2)}, u32[]{:S(2)}) async-start(bf16[8,12,4096]{2,1,0:T(8,128)(2,1)} %convert_element_type.72), calls=%async_computation.3 | async-start | bytes 2097152 | tf_op jit(solution)/shard_map/all_to_all | solution.py:173
  420.5 22.8 %all-to-all-done.1 = bf16[8,12,4096]{2,1,0:T(8,128)(2,1)S(1)} async-done(((bf16[8,12,4096]{2,1,0:T(8,128)(2,1)}), bf16[8,12,4096]{2,1,0:T(8,128)(2,1)S(1)}, u32[]{:S(2)}, u32[]{:S(2)}) %all-to-all-start.1) | async-done | bytes 786464 | tf_op jit(solution)/shard_map/all_to_all | solution.py:173
  443.3 1.4 reshape.143
  444.6 2.9 gather_fusion
  447.6 1.6 gather.7
  449.2 2.9 multiply_reduce_fusion.1
  452.1 1.7 fusion.15
  (217 shorter events, 78.0 us)
Async XLA Ops:
  7.2 8.9 %copy-start = (bf16[2048,544]{0,1:T(8,128)(2,1)S(1)}, bf16[2048,544]{0,1:T(8,128)(2,1)}, u32[]{:S(2)}) copy-start(bf16[2048,544]{0,1:T(8,128)(2,1)} %param.26) | copy-start | bytes 6684676
  7.2 43.9 %all-reduce.16.cloned.1.call-start = ((), (), s32[]{:S(2)}) async-start(), calls=%async_computation.4 | async-start | bytes 557056 | tf_op jit(solution)/shard_map/psum | solution.py:88
  8.1 4.5 collective-permute-start
  12.2 3.0 copy-start.12
  12.3 3.0 copy-start.14
  13.8 3.8 copy-start.11
  13.8 37.3 %copy-start.19 = (f32[2048]{0:T(1024)S(1)}, f32[2048]{0:T(1024)}, u32[]{:S(2)}) copy-start(f32[2048]{0:T(1024)} %param.28) | copy-start | bytes 24580
  15.3 0.8 copy-start.2
  17.6 130.3 %all-gather.6.cloned.1.call-start = ((), (), s32[]{:S(2)}) async-start(), calls=%async_computation.6 | async-start | bytes 1179648 | tf_op jit(solution)/shard_map/all_gather | solution.py:19
  98.0 7.1 %copy-start.9 = (f32[1,16,2048]{2,1,0:T(8,128)S(1)}, f32[1,16,2048]{2,1,0:T(8,128)}, u32[]{:S(2)}) copy-start(f32[1,16,2048]{2,1,0:T(8,128)} %slice.154) | copy-start | bytes 393220
  109.2 80.4 %all-gather.4.cloned.1.call-start = ((), (), s32[]{:S(2)}) async-start(), calls=%async_computation.5 | async-start | bytes 1179648 | tf_op jit(solution)/shard_map/all_gather | solution.py:19
  114.4 166.4 %reduce-scatter.3.cloned.1.call-start = ((), (), s32[]{:S(2)}) async-start(), calls=%async_computation.7 | async-start | bytes 2621440 | tf_op jit(solution)/shard_map/reduce_scatter | solution.py:128
  114.5 11.8 %copy-start.3 = (f32[8,16,2048]{2,1,0:T(8,128)S(1)}, f32[8,16,2048]{2,1,0:T(8,128)}, u32[]{:S(2)}) copy-start(f32[8,16,2048]{2,1,0:T(8,128)} %pad.102) | copy-start | bytes 3145732
  119.2 9.4 %copy-start.4 = (f32[8,16,2048]{2,1,0:T(8,128)S(1)}, f32[8,16,2048]{2,1,0:T(8,128)}, u32[]{:S(2)}) copy-start(f32[8,16,2048]{2,1,0:T(8,128)} %pad.45) | copy-start | bytes 3145732
  126.2 2.4 copy-start.5
  128.6 64.3 %copy-start.6 = (f32[7,16,2048]{2,1,0:T(8,128)S(1)}, f32[7,16,2048]{2,1,0:T(8,128)}, u32[]{:S(2)}) copy-start(f32[7,16,2048]{2,1,0:T(8,128)} %slice_add_fusion.5) | copy-start | bytes 2752516
  194.3 38.8 %copy-start.8 = (bf16[128,2048]{1,0:T(8,128)(2,1)S(1)}, bf16[128,2048]{1,0:T(8,128)(2,1)}, u32[]{:S(2)}) copy-start(bf16[128,2048]{1,0:T(8,128)(2,1)} %param.23) | copy-start | bytes 1572868
  194.3 38.8 %copy-start.13 = (f32[1,2048]{1,0:T(1,128)S(1)}, f32[1,2048]{1,0:T(1,128)}, u32[]{:S(2)}) copy-start(f32[1,2048]{1,0:T(1,128)} %copy-done.12) | copy-start | bytes 24580
  194.3 38.8 %copy-start.15 = (f32[1,2048]{1,0:T(1,128)S(1)}, f32[1,2048]{1,0:T(1,128)}, u32[]{:S(2)}) copy-start(f32[1,2048]{1,0:T(1,128)} %copy-done.14) | copy-start | bytes 24580
  194.3 38.8 %copy-start.16 = (f32[2048]{0:T(1024)S(1)}, f32[2048]{0:T(1024)}, u32[]{:S(2)}) copy-start(f32[2048]{0:T(1024)} %param.25) | copy-start | bytes 24580
  194.3 38.8 %copy-start.20 = (f32[2048]{0:T(1024)S(1)}, f32[2048]{0:T(1024)}, u32[]{:S(2)}) copy-start(f32[2048]{0:T(1024)} %param.30) | copy-start | bytes 24580
  234.1 9.6 %copy-start.18 = (s32[32,2]{0,1:T(2,128)S(1)}, s32[32,2]{0,1:T(2,128)}, u32[]{:S(2)}) copy-start(s32[32,2]{0,1:T(2,128)} %param.34) | copy-start | bytes 772
  234.2 46.7 %copy-start.10 = (bf16[32,4096]{1,0:T(8,128)(2,1)S(1)}, bf16[32,4096]{1,0:T(8,128)(2,1)}, u32[]{:S(2)}) copy-start(bf16[32,4096]{1,0:T(8,128)(2,1)} %param.32) | copy-start | bytes 786436
  243.7 39.1 %copy-start.17 = (f32[4096]{0:T(1024)S(1)}, f32[4096]{0:T(1024)}, u32[]{:S(2)}) copy-start(f32[4096]{0:T(1024)} %param.33) | copy-start | bytes 49156
  243.7 99.1 %all-gather.8.cloned.1.call-start = ((), (), s32[]{:S(2)}) async-start(), calls=%async_computation.8 | async-start | bytes 3932160 | tf_op jit(solution)/shard_map/all_gather | solution.py:163
  282.1 0.7 copy-start.7
  312.5 99.9 %reduce-scatter.5.cloned.1.call-start = ((), (), s32[]{:S(2)}) async-start(), calls=%async_computation.9 | async-start | bytes 3932160 | tf_op jit(solution)/shard_map/reduce_scatter | solution.py:167
  374.7 45.7 %copy-start.21 = (f32[32,2]{0,1:T(2,128)S(1)}, f32[32,2]{0,1:T(2,128)}, u32[]{:S(2)}) copy-start(f32[32,2]{0,1:T(2,128)} %param.35) | copy-start | bytes 772
  414.6 28.7 %all-to-all-start.1 = ((bf16[8,12,4096]{2,1,0:T(8,128)(2,1)}), bf16[8,12,4096]{2,1,0:T(8,128)(2,1)S(1)}, u32[]{:S(2)}, u32[]{:S(2)}) async-start(bf16[8,12,4096]{2,1,0:T(8,128)(2,1)} %convert_element_type.72), calls=%async_computation.3 | async-start | bytes 2097152 | tf_op jit(solution)/shard_map/all_to_all | solution.py:173
  444.6 9.1 %copy-start.1 = (bf16[2048,544]{0,1:T(8,128)(2,1)S(1)}, bf16[2048,544]{0,1:T(8,128)(2,1)}, u32[]{:S(2)}) copy-start(bf16[2048,544]{0,1:T(8,128)(2,1)} %param.26) | copy-start | bytes 6684676
Sparse Core Ops, SparseCore 0:
  17.7 33.3 all-reduce.15
  109.3 38.5 all-gather.5
  150.6 38.8 all-gather.3
  243.8 36.9 reduce-scatter.2
  312.6 30.0 all-gather.7
  374.9 37.5 reduce-scatter.4
where the time goes:
time: 467 us; the launch traced here: 461 us
  waiting for transfers between devices  220 us (47%)
  local copies, waits for them, and re-layouts  88.8 us (19%)
  other arithmetic  52.4 us (11%)
  matrix products  46.1 us (10%)
  blocking collectives  28 us (6%)
  between operations  14.6 us (3%)
  starting transfers between devices  9.1 us (2%)
    all_gather x2, waiting for transfers between devices, prefix(): gathered = jax.tree.map(lambda a: lax.all_gather(a, axis), part)  59.9 us
    reduce_scatter x1, waiting for transfers between devices, per_device(): lax.psum_scatter(expert_share(arrived_flat, up_weight, down_weight).astyp...  37.7 us
    reduce_scatter x1, waiting for transfers between devices, per_device(): lax.psum_scatter(jnp.dot(mixed, out_weight, preferred_element_type=jnp.fl...  36.2 us
    psum x1, waiting for transfers between devices, per_device(): lax.psum(jnp.dot(inner, x_weight, preferred_element_type=jnp.float32), 'tp')  33.4 us
    all_gather x1, waiting for transfers between devices, per_device(): lax.all_gather(arrived_seq.reshape(1, seq_count * capacity, width), 'tp',...  30 us
    mul x48, local copies, waits for them, and re-layouts, advance(): entry_row[:, :, None] * drive_row[:, None, :]  28.5 us
    all_to_all x1, blocking collectives, per_device(): lax.all_to_all(along_seq, 'seq', split_axis=0, concat_axis=0, tiled=True)  28 us
    all_to_all x1, waiting for transfers between devices, per_device(): lax.all_to_all(summed.reshape(seq_count, capacity, width).astype(jnp.bflo...  22.8 us
  transfers between devices with their start and end apart: 8, of which 8 were waited for; matrix products, arithmetic and copies ran while one was open for 5% of the time, Pallas kernels for 0%

commit v1 on v0

v1 whole, which is shorter than its diff:
```python
import functools

import jax
import jax.numpy as jnp
from jax import lax
from jax.experimental import pallas as pl
from jax.experimental.pallas import tpu as pltpu
from jax.sharding import PartitionSpec as P

STATE = 16
DTRANK = 512
EXPERTS = 8
MESH = pl.DeviceIdType.MESH
VMEM_SPEC = pl.BlockSpec(memory_space=pltpu.VMEM)
SMEM_SPEC = pl.BlockSpec(memory_space=pltpu.SMEM)
F32 = jnp.float32
BF16 = jnp.bfloat16
MIB = 1024 * 1024


def shifted(value, axis, steps):
    count = lax.axis_size(axis)
    initial, last = (max(0, -steps), min(count, count - steps))
    return lax.ppermute(value, axis, [(source, source + steps) for source in range(initial, last)])


def greet(peers):
    barrier = pltpu.get_barrier_semaphore()
    for peer in peers:
        pl.semaphore_signal(barrier, inc=1, device_id=peer, device_id_type=MESH)
    pl.semaphore_wait(barrier, len(peers))


def send(source, target, send_sem, recv_sem, device):
    return pltpu.make_async_remote_copy(
        src_ref=source,
        dst_ref=target,
        send_sem=send_sem,
        recv_sem=recv_sem,
        device_id=device,
        device_id_type=MESH,
    )


def bit_of(index, stage):
    return lax.rem(index // 2**stage, 2)


def flipped(index, stage):
    return index + 2**stage - 2 * 2**stage * bit_of(index, stage)


def stages_of(count):
    return count.bit_length() - 1


def sum_kernel(count, part_ref, out_ref, outgoing, arriving, send_sems, recv_sems):
    me = lax.axis_index("tp")
    stages = stages_of(count)
    greet([{"tp": flipped(me, k)} for k in range(stages)])
    for k in range(stages):
        source = part_ref if k == 0 else outgoing
        copy = send(
            source, arriving.at[k], send_sems.at[k], recv_sems.at[k], {"tp": flipped(me, k)}
        )
        copy.start()
        copy.wait()
        total = source[...].astype(F32) + arriving[k].astype(F32)
        if k < stages - 1:
            outgoing[...] = total.astype(BF16)
        else:
            out_ref[...] = total


def sum_over_tp(part):
    count = lax.axis_size("tp")
    stages = stages_of(count)
    return pl.pallas_call(
        functools.partial(sum_kernel, count),
        out_shape=jax.ShapeDtypeStruct(part.shape, F32),
        in_specs=[VMEM_SPEC],
        out_specs=VMEM_SPEC,
        scratch_shapes=[
            pltpu.VMEM(part.shape, BF16),
            pltpu.VMEM((stages, *part.shape), BF16),
            pltpu.SemaphoreType.DMA((stages,)),
            pltpu.SemaphoreType.DMA((stages,)),
        ],
        compiler_params=pltpu.CompilerParams(collective_id=0, has_side_effects=True),
        name="projection_sum",
    )(part)


def scan_kernel(
    count,
    step_ref,
    inner_ref,
    maps_ref,
    rate_ref,
    out_ref,
    state,
    outgoing,
    arriving,
    send_sems,
    recv_sems,
):
    me = lax.axis_index("seq")
    tokens = step_ref.shape[0]
    tile = step_ref.shape[1:]
    greet([{"seq": lax.rem(me + d, count)} for d in range(1, count)])

    def advance(t, states):
        step = step_ref[t]
        drive = step * inner_ref[t]
        return step, tuple(
            jnp.exp(step * rate_ref[n]) * states[n] + maps_ref[t, n] * drive for n in range(STATE)
        )

    def ending(t, carried):
        states, total = carried
        step, states = advance(t, states)
        return states, total + step

    zero = jnp.zeros(tile, F32)
    states, total = lax.fori_loop(0, tokens, ending, ((zero,) * STATE, zero))
    for n in range(STATE):
        outgoing[n] = states[n].astype(BF16)
    upper = total.astype(BF16)
    outgoing[STATE] = upper
    outgoing[STATE + 1] = (total - upper.astype(F32)).astype(BF16)

    def copy_by(d):
        return send(
            outgoing,
            arriving.at[d],
            send_sems.at[d],
            recv_sems.at[d],
            {"seq": lax.rem(me + d, count)},
        )

    for d in range(1, count):

        @pl.when(me + d < count)
        def _():
            copy_by(d).start()

    state[...] = jnp.zeros(state.shape, F32)
    for d in range(count - 1, 0, -1):

        @pl.when(me >= d)
        def _():
            copy_by(d).wait_recv()
            passed = arriving[d, STATE].astype(F32) + arriving[d, STATE + 1].astype(F32)
            for n in range(STATE):
                state[n] = jnp.exp(passed * rate_ref[n]) * state[n] + arriving[d, n].astype(F32)

    def reading(t, states):
        _, states = advance(t, states)
        terms = [maps_ref[t, STATE + n] * states[n] for n in range(STATE)]
        while len(terms) > 1:
            terms = [a + b for a, b in zip(terms[::2], terms[1::2])]
        out_ref[t] = terms[0]
        return states

    lax.fori_loop(0, tokens, reading, tuple(state[n] for n in range(STATE)))
    for d in range(1, count):

        @pl.when(me + d < count)
        def _():
            copy_by(d).wait_send()


def recur(step_size, inner, maps, decay_rate):
    count = lax.axis_size("seq")
    tokens, channels = step_size.shape
    tile = (channels // 128, 128)
    rate = -decay_rate.T.reshape(STATE, *tile)
    out = pl.pallas_call(
        functools.partial(scan_kernel, count),
        out_shape=jax.ShapeDtypeStruct((tokens, *tile), F32),
        in_specs=[VMEM_SPEC, VMEM_SPEC, SMEM_SPEC, VMEM_SPEC],
        out_specs=VMEM_SPEC,
        scratch_shapes=[
            pltpu.VMEM((STATE, *tile), F32),
            pltpu.VMEM((STATE + 2, *tile), BF16),
            pltpu.VMEM((count, STATE + 2, *tile), BF16),
            pltpu.SemaphoreType.DMA((count,)),
            pltpu.SemaphoreType.DMA((count,)),
        ],
        compiler_params=pltpu.CompilerParams(
            collective_id=1, has_side_effects=True, vmem_limit_bytes=24 * MIB
        ),
        name="recurrence",
    )(step_size.reshape(tokens, *tile), inner.reshape(tokens, *tile), maps, rate)
    return out.reshape(tokens, channels)


def mixer_kernel(count, part_ref, residual_ref, gain_ref, mixer_ref, normed_ref, *scratch):
    stages = stages_of(count)
    works, arrivings = scratch[:stages], scratch[stages : 2 * stages]
    send_sems, recv_sems, gather_send_sems, gather_recv_sems = scratch[2 * stages :]
    me = lax.axis_index("tp")
    greet([{"tp": flipped(me, k)} for k in range(stages)])
    total = None
    for k in range(stages):
        source = part_ref if k == 0 else works[k]
        kept = count // 2 ** (k + 1)
        bit = bit_of(me, k)
        copies = [
            send(
                source.at[2 * i + 1 - bit],
                arrivings[k].at[i],
                send_sems.at[k, i],
                recv_sems.at[k, i],
                {"tp": flipped(me, k)},
            )
            for i in range(kept)
        ]
        for copy in copies:
            copy.start()
        for i, copy in enumerate(copies):
            copy.wait()
            total = source[2 * i + bit].astype(F32) + arrivings[k][i].astype(F32)
            if k < stages - 1:
                works[k + 1][i] = total.astype(BF16)
    mixer = (total + residual_ref[...].astype(F32)).astype(BF16)
    mixer_ref[...] = mixer
    wide = mixer.astype(F32)
    normed_ref[me] = (
        wide
        * lax.rsqrt(jnp.mean(wide * wide, axis=1, keepdims=True) + 1e-06)
        * gain_ref[...]
    ).astype(BF16)
    for k in range(stages - 1, -1, -1):
        low = lax.rem(me, 2 ** (k + 1))
        copies = []
        for i in range(count // 2 ** (k + 1)):
            block = normed_ref.at[low + 2 ** (k + 1) * i]
            copies.append(
                send(
                    block,
                    block,
                    gather_send_sems.at[k, i],
                    gather_recv_sems.at[k, i],
                    {"tp": flipped(me, k)},
                )
            )
        for copy in copies:
            copy.start()
        for copy in copies:
            copy.wait()


def mixer_rows(part, residual, gain):
    count = lax.axis_size("tp")
    stages = stages_of(count)
    rows, width = residual.shape
    sems = pltpu.SemaphoreType.DMA((stages, count // 2))
    return pl.pallas_call(
        functools.partial(mixer_kernel, count),
        out_shape=(
            jax.ShapeDtypeStruct((rows, width), BF16),
            jax.ShapeDtypeStruct((count, rows, width), BF16),
        ),
        in_specs=[VMEM_SPEC] * 3,
        out_specs=(VMEM_SPEC, VMEM_SPEC),
        scratch_shapes=[pltpu.VMEM((count // 2**k, rows, width), BF16) for k in range(stages)]
        + [pltpu.VMEM((count // 2 ** (k + 1), rows, width), BF16) for k in range(stages)]
        + [sems] * 4,
        compiler_params=pltpu.CompilerParams(
            collective_id=2, has_side_effects=True, vmem_limit_bytes=32 * MIB
        ),
        name="mixer_sum",
    )(part.reshape(count, rows, width), residual, gain.reshape(1, width))


def expert_share(arrived_flat, up_weight, down_weight):
    hidden = jax.nn.silu(jnp.dot(arrived_flat, up_weight, preferred_element_type=F32)).astype(BF16)
    return jnp.dot(hidden, down_weight, preferred_element_type=F32).astype(BF16)


def per_device(
    x_in,
    gate_in,
    conv_weight,
    conv_bias,
    x_weight,
    dt_weight,
    dt_bias,
    decay_rate,
    skip_gain,
    out_weight,
    residual_in,
    norm_gain,
    expert_ids,
    gate_prob,
    up_weight,
    down_weight,
):
    tokens, channels = x_in.shape
    width = out_weight.shape[1]
    reach = conv_weight.shape[0] - 1
    rim_rows = shifted(x_in[tokens - reach :], "seq", 1)
    padded = jnp.concatenate([rim_rows, x_in], axis=0).astype(F32)
    conv_out = conv_bias[None, :] + sum(
        (
            conv_weight[offset][None, :] * padded[offset : offset + tokens]
            for offset in range(reach + 1)
        )
    )
    inner = jax.nn.silu(conv_out).astype(BF16)
    projected = sum_over_tp(jnp.dot(inner, x_weight, preferred_element_type=F32).astype(BF16))
    dt_low = projected[:, :DTRANK].astype(BF16)
    step_size = jax.nn.softplus(
        jnp.dot(dt_low, dt_weight, preferred_element_type=F32) + dt_bias[None, :]
    )
    ssm = recur(step_size, inner.astype(F32), projected[:, DTRANK:], decay_rate)
    mixed = (
        (ssm + skip_gain[None, :] * inner.astype(F32)) * jax.nn.silu(gate_in.astype(F32))
    ).astype(BF16)
    rows = tokens // lax.axis_size("tp")
    mixer_out, normed_all = mixer_rows(
        jnp.dot(mixed, out_weight, preferred_element_type=F32).astype(BF16), residual_in, norm_gain
    )
    normed = lax.dynamic_index_in_dim(normed_all, lax.axis_index("tp"), 0, False)
    mixer_wide = mixer_out.astype(F32)
    seq_count = lax.axis_size("seq")
    devices = seq_count * lax.axis_size("tp")
    seq_group = seq_count // EXPERTS
    capacity = 3 * rows // EXPERTS
    chosen = expert_ids.reshape(-1)
    expert_hits = (chosen[:, None] == jnp.arange(EXPERTS, dtype=jnp.int32)[None, :]).astype(
        jnp.int32
    )
    earlier_hits = jnp.cumsum(expert_hits, axis=0) - expert_hits
    slot_index = jnp.sum(earlier_hits * expert_hits, axis=1)
    target = chosen * capacity + slot_index
    placing = (jnp.arange(EXPERTS * capacity, dtype=jnp.int32)[:, None] == target[None, :]).astype(
        jnp.bfloat16
    )
    placing = jnp.sum(placing.reshape(EXPERTS * capacity, rows, 2), axis=2)
    slots_out = (
        jnp.dot(placing, normed, preferred_element_type=jnp.float32)
        .astype(jnp.bfloat16)
        .reshape(EXPERTS, capacity, width)
    )
    along_seq = jnp.repeat(slots_out, seq_group, axis=0)
    arrived_seq = lax.all_to_all(along_seq, "seq", split_axis=0, concat_axis=0, tiled=True)
    arrived_all = lax.all_gather(
        arrived_seq.reshape(1, seq_count * capacity, width), "tp", axis=0, tiled=True
    )
    arrived_flat = arrived_all.reshape(devices * capacity, width)
    summed = lax.psum_scatter(
        expert_share(arrived_flat, up_weight, down_weight).astype(jnp.float32).astype(jnp.bfloat16),
        "tp",
        scatter_dimension=0,
        tiled=True,
    ).astype(jnp.float32)
    home = lax.all_to_all(
        summed.reshape(seq_count, capacity, width).astype(jnp.bfloat16),
        "seq",
        split_axis=0,
        concat_axis=0,
        tiled=True,
    ).astype(jnp.float32)
    expert_out = jnp.sum(home.reshape(EXPERTS, seq_group, capacity, width), axis=1).reshape(
        EXPERTS * capacity, width
    )
    picked = jnp.take(expert_out, target, axis=0).reshape(rows, 2, width)
    layer_out = (mixer_wide + jnp.sum(picked * gate_prob[:, :, None], axis=1)).astype(jnp.bfloat16)
    return (mixer_out, layer_out)


def solution(mesh):
    return jax.shard_map(
        per_device,
        mesh=mesh,
        in_specs=(
            P("seq", "tp"),
            P("seq", "tp"),
            P(None, "tp"),
            P("tp"),
            P("tp", None),
            P(None, "tp"),
            P("tp"),
            P("tp", None),
            P("tp"),
            P("tp", None),
            P(("seq", "tp"), None),
            P(),
            P(("seq", "tp"), None),
            P(("seq", "tp"), None),
            P(None, ("seq", "tp")),
            P(("seq", "tp"), None),
        ),
        out_specs=(P(("seq", "tp"), None), P(("seq", "tp"), None)),
        check_vma=False,
    )
```

time: 467 us -> 276 us (0.59)
  waiting for transfers between devices: 220 us -> 89.1 us
  local copies, waits for them, and re-layouts: 88.8 us -> 16.9 us
  Pallas kernels: 0 us -> 53.2 us
  other arithmetic: 52.4 us -> 9.39 us
  blocking collectives: 28 us -> 35.7 us
    all_gather x2 -> x0, waiting for transfers between devices: 59.9 us -> none  [prefix(): gathered = jax.tree.map(lambda a: lax.all_gather(a, axis), part)]
    pallas_call x0 -> x3, Pallas kernels: none -> 53.2 us  [the longest x1 22.3 us: mixer_rows(): pl.pallas_call(functools.partial(mixer_kernel, count), out_shape=(jax.Sha...]
    reduce_scatter x1 -> x0, waiting for transfers between devices: 36.2 us -> none  [per_device(): lax.psum_scatter(jnp.dot(mixed, out_weight, preferred_element_type=jnp.fl...]
    psum x1 -> x0, waiting for transfers between devices: 33.4 us -> none  [per_device(): lax.psum(jnp.dot(inner, x_weight, preferred_element_type=jnp.float32), 'tp')]
    mul x64 -> x0, local copies, waits for them, and re-layouts: 28.6 us -> none  [the longest x48 28.5 us: advance(): entry_row[:, :, None] * drive_row[:, None, :]]
    add x27 -> x0, other arithmetic: 22.2 us -> none  [the longest x7 9.82 us: per_device(): lax.associative_scan(chain_join, (block_decay, block_ends), axis=0)]
    pad x7 -> x0, local copies, waits for them, and re-layouts: 18.7 us -> none  [per_device(): lax.associative_scan(chain_join, (block_decay, block_ends), axis=0)]
    reduce_sum x18 -> x0, other arithmetic: 14 us -> none  [the longest x16 12.2 us: advance(): return (carried, jnp.sum(readout_row[:, :, None] * carried, axis=1))]
  transfers between devices with their start and end apart: 8 -> 4, of which waited for: 8 -> 3; matrix products, arithmetic and copies ran while one was open for 5% -> 2% of each run, Pallas kernels for 0% -> 0%
where the time goes in v1:
time: 276 us; the launch traced here: 272 us
  waiting for transfers between devices  89.1 us (32%)
  Pallas kernels  53.2 us (19%)
  matrix products  44.1 us (16%)
  blocking collectives  35.7 us (13%)
  local copies, waits for them, and re-layouts  16.9 us (6%)
  between operations  14.3 us (5%)
  other arithmetic  9.39 us (3%)
  starting transfers between devices  8.89 us (3%)
    reduce_scatter x1, waiting for transfers between devices, per_device(): lax.psum_scatter(expert_share(arrived_flat, up_weight, down_weight).astyp...  37.7 us
    all_to_all x1, blocking collectives, per_device(): lax.all_to_all(along_seq, 'seq', split_axis=0, concat_axis=0, tiled=True)  35.7 us
    all_gather x1, waiting for transfers between devices, per_device(): lax.all_gather(arrived_seq.reshape(1, seq_count * capacity, width), 'tp',...  29.8 us
    pallas_call x1, Pallas kernels, mixer_rows(): pl.pallas_call(functools.partial(mixer_kernel, count), out_shape=(jax.Sha...  22.3 us
    all_to_all x1, waiting for transfers between devices, per_device(): lax.all_to_all(summed.reshape(seq_count, capacity, width).astype(jnp.bflo...  21.6 us
    pallas_call x1, Pallas kernels, recur(): pl.pallas_call(functools.partial(scan_kernel, count), out_shape=jax.Shape...  21.1 us
    dot_general x1, matrix products, expert_share(): jnp.dot(arrived_flat, up_weight, preferred_element_type=F32)  16.1 us
    dot_general x1, matrix products, expert_share(): return jnp.dot(hidden, down_weight, preferred_element_type=F32).astype(BF16)  15.9 us
  transfers between devices with their start and end apart: 4, of which 3 were waited for; matrix products, arithmetic and copies ran while one was open for 2% of the time, Pallas kernels for 0%

profile of v1, /device:TPU:13, one launch (start us, length us, event | category | flops | bytes accessed | tf_op | source)
XLA Modules:
  0.0 271.5 jit_solution(18427477389381453053)
XLA Ops:
  7.2 0.9 slice.35
  8.1 3.1 %collective-permute-start = (bf16[3,2048]{1,0:T(4,128)(2,1)S(1)}, bf16[3,2048]{1,0:T(4,128)(2,1)S(1)}, u32[]{:S(2)}, u32[]{:S(2)}) collective-permute-start(bf16[3,2048]{1,0:T(4,128)(2,1)S(1)} %slice.35), channel_id=1, source_target_pairs={{0,4},{4,8},{8,12},{12,16},{16,20},{20,24},{24,28},{1,5},{5,9},{9,... | collective-permute-start | bytes 36872 | tf_op jit(solution)/shard_map/ppermute | solution.py:24
  11.3 0.9 fusion.26
  12.2 0.9 negate_bitcast_fusion
  13.2 0.8 copy.36
  13.9 0.1 reshape.111
  14.1 0.1 reduce_window_sum.11
  14.2 0.2 select_reduce_fusion
  14.4 0.1 reduce_sum.39
  14.5 0.1 copy.37
  14.6 1.2 compare_and_fusion
  15.8 0.1 fusion.19
  15.9 1.2 maximum_convert_fusion
  17.1 1.4 convert_bitcast_fusion
  18.5 0.8 copy-done.4
  19.3 0.7 convolution_convert_fusion.3
  20.1 0.8 copy.35.part_ref
  20.9 9.8 %projection_sum.1 = f32[128,544]{1,0:T(8,128)} custom-call(bf16[128,544]{1,0:T(8,128)(2,1)} %copy.35.part_ref), custom_call_target="tpu_custom_call" | custom-call | tf_op jit(solution)/shard_map/projection_sum/pallas_call | solution.py:78
  30.6 0.8 slice.44.maps_ref
  31.5 2.5 fusion.7
  34.0 0.2 copy.41
  34.2 0.2 copy.42
  34.4 21.1 %recurrence.1 = f32[128,16,128]{2,1,0:T(8,128)S(1)} custom-call(f32[128,16,128]{2,1,0:T(8,128)S(1)} %bitcast.46, f32[128,16,128]{2,1,0:T(8,128)S(1)} %bitcast.47, f32[128,32]{1,0:T(8,128)S(1)} %slice.44.maps_ref, f32[16,16,128]{2,1,0:T(8,128)S(1)} %bitcast.50), custom_call_target="tpu_custom_call" | custom-call | tf_op jit(solution)/shard_map/recurrence/pallas_call | solution.py:178
  55.6 8.6 %convolution_convert_fusion.1 = bf16[128,4096]{1,0:T(8,128)(2,1)S(1)} fusion(bf16[2048,4096]{1,0:T(8,128)(2,1)} %param.25, bf16[128,2048]{1,0:T(8,128)(2,1)S(1)} %copy-done.5, bf16[128,2048]{1,0:T(8,128)(2,1)S(1)} %copy-done.11, f32[16,8,16,128]{3,2,1,0:T(8,128)S(1)} %bitcast.48, f32[2048]{0:T(1024)S(1)} %copy-done.12), kind=kOutput, calls=%fused_computation.2 | convolution fusion | flops 2150629376 | bytes 19931136 | tf_op jit(solution)/shard_map/dot_general | solution.py:323
  64.2 22.3 %mixer_sum.1 = (bf16[32,4096]{1,0:T(8,128)(2,1)S(1)}, bf16[4,32,4096]{2,1,0:T(8,128)(2,1)S(1)}) custom-call(bf16[4,32,4096]{2,1,0:T(8,128)(2,1)S(1)} %bitcast.49, bf16[32,4096]{1,0:T(8,128)(2,1)S(1)} %copy-done.2, f32[1,4096]{1,0:T(1,128)S(1)} %bitcast.51), custom_call_target="tpu_custom_call" | custom-call | tf_op jit(solution)/shard_map/mixer_sum/pallas_call | solution.py:259
  86.4 0.4 convolution_convert_fusion.2
  86.8 0.2 reshape_broadcast_in_dim_reshape.3
  87.0 35.7 %all_to_all.10 = bf16[8,12,4096]{2,1,0:T(8,128)(2,1)S(1)} all-to-all(bf16[8,12,4096]{2,1,0:T(8,128)(2,1)S(1)} %reshape_broadcast_in_dim_reshape.3), channel_id=1, replica_groups=mesh['seq'=8,'tp'=4] {'seq'}, dimensions={0} | all-to-all | bytes 1572864 | tf_op jit(solution)/shard_map/all_to_all | solution.py:348
  122.7 1.1 reshape.112
  123.8 0.2 reduce-scatter.2.cloned.1.call-start
  124.0 29.8 %all-gather.2.cloned.1.call-done = bf16[4,96,4096]{2,1,0:T(8,128)(2,1)} async-done(((bf16[1,96,4096]{2,1,0:T(8,128)(2,1)}), bf16[4,96,4096]{2,1,0:T(8,128)(2,1)}) %all-gather.2.cloned.1.call-update) | async-done | bytes 3145744 | tf_op jit(solution)/shard_map/all_gather | solution.py:349
  153.8 16.1 %multiply_convert_fusion.6 = bf16[384,3072]{1,0:T(8,128)(2,1)S(1)} fusion(bf16[384,4096]{1,0:T(8,128)(2,1)} %bitcast.56, bf16[4096,3072]{1,0:T(8,128)(2,1)} %param.30), kind=kOutput, calls=%fused_computation.3.clone.clone.1 | convolution fusion | flops 9669574656 | bytes 30670848 | tf_op jit(solution)/shard_map/dot_general | solution.py:278
  169.9 15.9 %convolution_convert_fusion = bf16[384,4096]{1,0:T(8,128)(2,1)} fusion(bf16[3072,4096]{1,0:T(8,128)(2,1)} %param.31, bf16[384,3072]{1,0:T(8,128)(2,1)S(1)} %multiply_convert_fusion.6), kind=kOutput, calls=%fused_computation.1 | convolution fusion | flops 9665249280 | bytes 30670848 | tf_op jit(solution)/shard_map/dot_general | solution.py:279
  185.8 37.7 %reduce-scatter.2.cloned.1.call-done = bf16[96,4096]{1,0:T(8,128)(2,1)} async-done(((bf16[384,4096]{1,0:T(8,128)(2,1)}), bf16[96,4096]{1,0:T(8,128)(2,1)}) %reduce-scatter.2.cloned.1.call-update) | async-done | bytes 786448 | tf_op jit(solution)/shard_map/reduce_scatter | solution.py:353
  223.5 2.2 convert_element_type.68
  225.7 5.5 %all-to-all-start.1 = ((bf16[8,12,4096]{2,1,0:T(8,128)(2,1)}), bf16[8,12,4096]{2,1,0:T(8,128)(2,1)S(1)}, u32[]{:S(2)}, u32[]{:S(2)}) async-start(bf16[8,12,4096]{2,1,0:T(8,128)(2,1)} %convert_element_type.68), calls=%async_computation.2 | async-start | bytes 2097152 | tf_op jit(solution)/shard_map/all_to_all | solution.py:359
  231.2 0.1 copy.39
  231.2 0.1 mul.117
  231.4 0.7 copy.38
  232.1 0.1 copy.40
  232.1 0.6 pad_clamp_fusion
  232.8 21.6 %all-to-all-done.1 = bf16[8,12,4096]{2,1,0:T(8,128)(2,1)S(1)} async-done(((bf16[8,12,4096]{2,1,0:T(8,128)(2,1)}), bf16[8,12,4096]{2,1,0:T(8,128)(2,1)S(1)}, u32[]{:S(2)}, u32[]{:S(2)}) %all-to-all-start.1) | async-done | bytes 786464 | tf_op jit(solution)/shard_map/all_to_all | solution.py:359
  254.3 1.3 reshape.117
  255.7 3.1 %gather_fusion = f32[64,4096]{1,0:T(8,128)S(1)} fusion(f32[96,4096]{1,0:T(8,128)} %reshape.117, s32[1024]{0:T(1024)} %pad_clamp_fusion), kind=kCustom, calls=%fused_computation | custom fusion | bytes 2097408 | tf_op jit(solution)/shard_map/jit(_take)/gather | solution.py:369
  258.7 1.6 gather.7
  260.3 2.9 %multiply_reduce_fusion = f32[32,4096]{1,0:T(8,128)S(1)} fusion(f32[32,2,4096]{2,1,0:T(2,128)} %gather.7, pred[32,2]{1,0:T(8,128)(4,1)} %copy.38, f32[32,2]{1,0:T(8,128)S(1)} %copy.40), kind=kLoop, calls=%fused_computation.28 | loop fusion | flops 655360 | bytes 1573184 | tf_op jit(solution)/shard_map/reduce_sum | solution.py:370
  263.2 0.8 add_convert_fusion
  264.0 0.7 copy.48
  (33 shorter events, 0.2 us)
Async XLA Ops:
  7.2 12.1 %copy-start = (bf16[2048,544]{0,1:T(8,128)(2,1)S(1)}, bf16[2048,544]{0,1:T(8,128)(2,1)}, u32[]{:S(2)}) copy-start(bf16[2048,544]{0,1:T(8,128)(2,1)} %param.20) | copy-start | bytes 6684676
  7.2 146.6 %all-gather.2.cloned.1.call-start = ((), (), s32[]{:S(2)}) async-start(), calls=%async_computation.3 | async-start | bytes 3932160 | tf_op jit(solution)/shard_map/all_gather | solution.py:349
  8.1 7.8 %collective-permute-start = (bf16[3,2048]{1,0:T(4,128)(2,1)S(1)}, bf16[3,2048]{1,0:T(4,128)(2,1)S(1)}, u32[]{:S(2)}, u32[]{:S(2)}) collective-permute-start(bf16[3,2048]{1,0:T(4,128)(2,1)S(1)} %slice.35), channel_id=1, source_target_pairs={{0,4},{4,8},{8,12},{12,16},{16,20},{20,24},{24,28},{1,5},{5,9},{9,... | collective-permute-start | bytes 36872 | tf_op jit(solution)/shard_map/ppermute | solution.py:24
  14.4 1.5 copy-start.7
  18.5 0.8 copy-start.4
  34.2 21.4 %copy-start.5 = (bf16[128,2048]{1,0:T(8,128)(2,1)S(1)}, bf16[128,2048]{1,0:T(8,128)(2,1)}, u32[]{:S(2)}) copy-start(bf16[128,2048]{1,0:T(8,128)(2,1)} %copy-done.4) | copy-start | bytes 1572868
  34.2 21.4 %copy-start.11 = (bf16[128,2048]{1,0:T(8,128)(2,1)S(1)}, bf16[128,2048]{1,0:T(8,128)(2,1)}, u32[]{:S(2)}) copy-start(bf16[128,2048]{1,0:T(8,128)(2,1)} %param.17) | copy-start | bytes 1572868
  34.2 21.4 %copy-start.12 = (f32[2048]{0:T(1024)S(1)}, f32[2048]{0:T(1024)}, u32[]{:S(2)}) copy-start(f32[2048]{0:T(1024)} %param.24) | copy-start | bytes 24580
  55.6 8.6 %copy-start.2 = (bf16[32,4096]{1,0:T(8,128)(2,1)S(1)}, bf16[32,4096]{1,0:T(8,128)(2,1)}, u32[]{:S(2)}) copy-start(bf16[32,4096]{1,0:T(8,128)(2,1)} %residual_ref.1) | copy-start | bytes 786436
  55.6 8.6 %copy-start.3 = (f32[4096]{0:T(1024)S(1)}, f32[4096]{0:T(1024)}, u32[]{:S(2)}) copy-start(f32[4096]{0:T(1024)} %param.27) | copy-start | bytes 49156
  123.8 99.7 %reduce-scatter.2.cloned.1.call-start = ((), (), s32[]{:S(2)}) async-start(), calls=%async_computation.4 | async-start | bytes 3932160 | tf_op jit(solution)/shard_map/reduce_scatter | solution.py:353
  185.8 45.4 %copy-start.6 = (s32[32,2]{0,1:T(2,128)S(1)}, s32[32,2]{0,1:T(2,128)}, u32[]{:S(2)}) copy-start(s32[32,2]{0,1:T(2,128)} %param.28) | copy-start | bytes 772
  185.8 45.6 %copy-start.9 = (pred[32,2]{0,1:T(4,128)(4,1)S(1)}, pred[32,2]{0,1:T(4,128)(4,1)}, u32[]{:S(2)}) copy-start(pred[32,2]{0,1:T(4,128)(4,1)} %get-tuple-element.6) | copy-start | bytes 196
  185.8 46.3 %copy-start.10 = (f32[32,2]{0,1:T(2,128)S(1)}, f32[32,2]{0,1:T(2,128)}, u32[]{:S(2)}) copy-start(f32[32,2]{0,1:T(2,128)} %param.29) | copy-start | bytes 772
  185.8 46.4 %copy-start.8 = (s32[64]{0:T(128)S(1)}, s32[64]{0:T(128)}, u32[]{:S(2)}) copy-start(s32[64]{0:T(128)} %copy-done.7) | copy-start | bytes 772
  225.7 28.7 %all-to-all-start.1 = ((bf16[8,12,4096]{2,1,0:T(8,128)(2,1)}), bf16[8,12,4096]{2,1,0:T(8,128)(2,1)S(1)}, u32[]{:S(2)}, u32[]{:S(2)}) async-start(bf16[8,12,4096]{2,1,0:T(8,128)(2,1)} %convert_element_type.68), calls=%async_computation.2 | async-start | bytes 2097152 | tf_op jit(solution)/shard_map/all_to_all | solution.py:359
  255.7 9.0 %copy-start.1 = (bf16[2048,544]{0,1:T(8,128)(2,1)S(1)}, bf16[2048,544]{0,1:T(8,128)(2,1)}, u32[]{:S(2)}) copy-start(bf16[2048,544]{0,1:T(8,128)(2,1)} %param.20) | copy-start | bytes 6684676
Sparse Core Ops, SparseCore 0:
  123.9 29.8 all-gather.1
  185.9 37.5 reduce-scatter.1

commit v2 on v1

--- a/solution.py
+++ b/solution.py
@@ -198,9 +198,9 @@
 def mixer_kernel(count, part_ref, residual_ref, gain_ref, mixer_ref, normed_ref, *scratch):
     stages = stages_of(count)
     works, arrivings = scratch[:stages], scratch[stages : 2 * stages]
-    send_sems, recv_sems, gather_send_sems, gather_recv_sems = scratch[2 * stages :]
+    columns, send_sems, recv_sems, gather_send_sems, gather_recv_sems = scratch[2 * stages :]
     me = lax.axis_index("tp")
-    greet([{"tp": flipped(me, k)} for k in range(stages)])
+    greet([{"tp": lax.rem(me + d, count)} for d in range(1, count)])
     total = None
     for k in range(stages):
         source = part_ref if k == 0 else works[k]
@@ -226,29 +226,29 @@
     mixer = (total + residual_ref[...].astype(F32)).astype(BF16)
     mixer_ref[...] = mixer
     wide = mixer.astype(F32)
-    normed_ref[me] = (
-        wide
-        * lax.rsqrt(jnp.mean(wide * wide, axis=1, keepdims=True) + 1e-06)
-        * gain_ref[...]
+    normed = (
+        wide * lax.rsqrt(jnp.mean(wide * wide, axis=1, keepdims=True) + 1e-06) * gain_ref[...]
     ).astype(BF16)
-    for k in range(stages - 1, -1, -1):
-        low = lax.rem(me, 2 ** (k + 1))
-        copies = []
-        for i in range(count // 2 ** (k + 1)):
-            block = normed_ref.at[low + 2 ** (k + 1) * i]
-            copies.append(
-                send(
-                    block,
-                    block,
-                    gather_send_sems.at[k, i],
-                    gather_recv_sems.at[k, i],
-                    {"tp": flipped(me, k)},
-                )
+    part_width = columns.shape[2]
+    for j in range(count):
+        columns[j] = normed[:, j * part_width : (j + 1) * part_width]
+    copies = []
+    for d in range(1, count):
+        peer = lax.rem(me + d, count)
+        copies.append(
+            send(
+                columns.at[peer],
+                normed_ref.at[me],
+                gather_send_sems.at[d],
+                gather_recv_sems.at[d],
+                {"tp": peer},
             )
-        for copy in copies:
-            copy.start()
-        for copy in copies:
-            copy.wait()
+        )
+    for copy in copies:
+        copy.start()
+    normed_ref[me] = columns[me]
+    for copy in copies:
+        copy.wait()
 
 
 def mixer_rows(part, residual, gain):
@@ -260,13 +260,15 @@
         functools.partial(mixer_kernel, count),
         out_shape=(
             jax.ShapeDtypeStruct((rows, width), BF16),
-            jax.ShapeDtypeStruct((count, rows, width), BF16),
+            jax.ShapeDtypeStruct((count, rows, width // count), BF16),
         ),
         in_specs=[VMEM_SPEC] * 3,
         out_specs=(VMEM_SPEC, VMEM_SPEC),
         scratch_shapes=[pltpu.VMEM((count // 2**k, rows, width), BF16) for k in range(stages)]
         + [pltpu.VMEM((count // 2 ** (k + 1), rows, width), BF16) for k in range(stages)]
-        + [sems] * 4,
+        + [pltpu.VMEM((count, rows, width // count), BF16)]
+        + [sems] * 2
+        + [pltpu.SemaphoreType.DMA((count,))] * 2,
         compiler_params=pltpu.CompilerParams(
             collective_id=2, has_side_effects=True, vmem_limit_bytes=32 * MIB
         ),
@@ -274,9 +276,247 @@
     )(part.reshape(count, rows, width), residual, gain.reshape(1, width))
 
 
+def dispatch_kernel(
+    count,
+    lanes,
+    group,
+    placing_ref,
+    normed_ref,
+    out_ref,
+    slots,
+    send_sems,
+    recv_sems,
+    spread_send_sems,
+    spread_recv_sems,
+):
+    me, lane = lax.axis_index("seq"), lax.axis_index("tp")
+    stages = stages_of(lanes)
+    capacity, part_width = slots.shape[1:]
+    greet(
+        [{"seq": lax.rem(me + d, count)} for d in range(1, count)]
+        + [{"tp": flipped(lane, k)} for k in range(stages)]
+    )
+
+    def block(source, column):
+        return (
+            pl.ds(pl.multiple_of(source * capacity, 16), capacity),
+            pl.ds(pl.multiple_of(column * part_width, 128), part_width),
+        )
+
+    placed = jnp.dot(placing_ref[...], normed_ref[...], preferred_element_type=F32).astype(BF16)
+    for e in range(EXPERTS):
+        slots[e] = placed[e * capacity : (e + 1) * capacity]
+    firsts = []
+    for d in range(1, count):
+        target = lax.rem(me + d, count)
+        firsts.append(
+            send(
+                slots.at[target // group],
+                out_ref.at[block(me, lane)],
+                send_sems.at[d],
+                recv_sems.at[d],
+                {"seq": target},
+            )
+        )
+        firsts[-1].start()
+    out_ref[block(me, lane)] = slots[me // group]
+
+    spread = {}
+    for step in range(count + stages - 1):
+        for k in range(stages - 1, -1, -1):
+            d = step - (stages - 1 - k)
+            if d < 0 or d >= count:
+                continue
+            if k == stages - 1:
+                if d > 0:
+                    firsts[d - 1].wait_recv()
+            else:
+                for copy in spread[d, k + 1]:
+                    copy.wait_recv()
+            source = lax.rem(me - d + count, count)
+            low = lax.rem(lane, 2 ** (k + 1))
+            spread[d, k] = []
+            for i in range(lanes // 2 ** (k + 1)):
+                place = out_ref.at[block(source, low + 2 ** (k + 1) * i)]
+                copy = send(
+                    place,
+                    place,
+                    spread_send_sems.at[d, k, i],
+                    spread_recv_sems.at[d, k, i],
+                    {"tp": flipped(lane, k)},
+                )
+                copy.start()
+                spread[d, k].append(copy)
+    for copy in firsts:
+        copy.wait_send()
+    for (_, k), copies in spread.items():
+        for copy in copies:
+            copy.wait_send()
+            if k == 0:
+                copy.wait_recv()
+
+
+def dispatch(placing, normed, group):
+    count, lanes = lax.axis_size("seq"), lax.axis_size("tp")
+    stages = stages_of(lanes)
+    capacity = placing.shape[0] // EXPERTS
+    part_width = normed.shape[1]
+    return pl.pallas_call(
+        functools.partial(dispatch_kernel, count, lanes, group),
+        out_shape=jax.ShapeDtypeStruct((count * capacity, lanes * part_width), BF16),
+        in_specs=[VMEM_SPEC] * 2,
+        out_specs=VMEM_SPEC,
+        scratch_shapes=[pltpu.VMEM((EXPERTS, capacity, part_width), BF16)]
+        + [pltpu.SemaphoreType.DMA((count,))] * 2
+        + [pltpu.SemaphoreType.DMA((count, stages, lanes // 2))] * 2,
+        compiler_params=pltpu.CompilerParams(
+            collective_id=3, has_side_effects=True, vmem_limit_bytes=32 * MIB
+        ),
+        name="dispatch",
+    )(placing, normed)
+
+
+def return_kernel(
+    count, lanes, part_ref, pick_ref, prob_ref, mixer_ref, out_ref, *scratch
+):
+    stages = stages_of(lanes)
+    works, arrivings = scratch[:stages], scratch[stages : 2 * stages]
+    home, outgoing, incoming = scratch[2 * stages : 2 * stages + 3]
+    sum_send, sum_recv, home_send, home_recv, row_send, row_recv = scratch[2 * stages + 3 :]
+    me, lane = lax.axis_index("seq"), lax.axis_index("tp")
+    capacity, part_width = home.shape[1:]
+    greet(
+        [{"seq": lax.rem(me + d, count)} for d in range(1, count)]
+        + [{"tp": lax.rem(lane + d, lanes)} for d in range(1, lanes)]
+    )
+
+    def block(d, column):
+        target = lax.rem(me + d, count)
+        return (
+            pl.ds(pl.multiple_of(target * capacity, 16), capacity),
+            pl.ds(pl.multiple_of(column * part_width, 128), part_width),
+        )
+
+    def start(d, k):
+        bit = bit_of(lane, k)
+        copies = []
+        for i in range(lanes // 2 ** (k + 1)):
+            index = 2 * i + 1 - bit
+            source = part_ref.at[block(d, index)] if k == 0 else works[k - 1].at[d, index]
+            copy = send(
+                source,
+                arrivings[k].at[d, i],
+                sum_send.at[d, k, i],
+                sum_recv.at[d, k, i],
+                {"tp": flipped(lane, k)},
+            )
+            copy.start()
+            copies.append(copy)
+        return copies
+
+    def finish(d, k, copies):
+        bit = bit_of(lane, k)
+        for i, copy in enumerate(copies):
+            copy.wait_recv()
+            index = 2 * i + bit
+            mine = part_ref[block(d, index)] if k == 0 else works[k - 1][d, index]
+            works[k][d, i] = (mine.astype(F32) + arrivings[k][d, i].astype(F32)).astype(BF16)
+
+    order = list(range(1, count)) + [0]
+    sums = {(d, 0): start(d, 0) for d in order}
+    homes = []
+    for step in range(count + stages - 1):
+        for k in range(stages):
+            if step - k < 0 or step - k >= count:
+                continue
+            d = order[step - k]
+            finish(d, k, sums[d, k])
+            if k < stages - 1:
+                sums[d, k + 1] = start(d, k + 1)
+            elif d == 0:
+                home[me] = works[k][0, 0]
+            else:
+                copy = send(
+                    works[k].at[d, 0],
+                    home.at[me],
+                    home_send.at[d],
+                    home_recv.at[d],
+                    {"seq": lax.rem(me + d, count)},
+                )
+                copy.start()
+                homes.append(copy)
+    for copy in homes:
+        copy.wait_recv()
+    arrived = home[...].reshape(count * capacity, part_width)
+    picked = jnp.dot(pick_ref[...], arrived, preferred_element_type=F32) * prob_ref[...]
+    half = picked.shape[0] // 2
+    outgoing[...] = (picked[:half] + picked[half:]).astype(BF16).reshape(outgoing.shape)
+    rows = []
+    for d in range(1, lanes):
+        peer = lax.rem(lane + d, lanes)
+        copy = send(
+            outgoing.at[peer], incoming.at[lane], row_send.at[d], row_recv.at[d], {"tp": peer}
+        )
+        copy.start()
+        rows.append(copy)
+    incoming[lane] = outgoing[lane]
+    for copy in rows:
+        copy.wait()
+    for j in range(lanes):
+        span = slice(j * part_width, (j + 1) * part_width)
+        out_ref[:, span] = (mixer_ref[:, span].astype(F32) + incoming[j].astype(F32)).astype(BF16)
+    for copy in homes:
+        copy.wait_send()
+    for copies in sums.values():
+        for copy in copies:
+            copy.wait_send()
+
+
+def bring_back(part, pick, prob, mixer):
+    count, lanes = lax.axis_size("seq"), lax.axis_size("tp")
+    stages = stages_of(lanes)
+    rows, width = mixer.shape
+    block = (part.shape[0] // count, width // lanes)
+    sums = [
+        pltpu.VMEM((count, lanes // 2 ** (k + 1), *block), BF16) for _ in range(2) for k in range(stages)
+    ]
+    return pl.pallas_call(
+        functools.partial(return_kernel, count, lanes),
+        out_shape=jax.ShapeDtypeStruct((rows, width), BF16),
+        in_specs=[VMEM_SPEC] * 4,
+        out_specs=VMEM_SPEC,
+        scratch_shapes=sums
+        + [pltpu.VMEM((count, *block), BF16)]
+        + [pltpu.VMEM((lanes, rows, block[1]), BF16)] * 2
+        + [pltpu.SemaphoreType.DMA((count, stages, lanes // 2))] * 2
+        + [pltpu.SemaphoreType.DMA((count,))] * 2
+        + [pltpu.SemaphoreType.DMA((lanes,))] * 2,
+        compiler_params=pltpu.CompilerParams(
+            collective_id=4, has_side_effects=True, vmem_limit_bytes=40 * MIB
+        ),
+        name="bring_back",
+    )(part, pick, prob, mixer)
+
+
 def expert_share(arrived_flat, up_weight, down_weight):
     hidden = jax.nn.silu(jnp.dot(arrived_flat, up_weight, preferred_element_type=F32)).astype(BF16)
     return jnp.dot(hidden, down_weight, preferred_element_type=F32).astype(BF16)
+
+
+def routing(expert_ids, gate_prob):
+    rows = expert_ids.shape[0]
+    lanes = lax.axis_size("tp")
+    capacity = 3 * rows // EXPERTS
+    both = lax.all_gather(
+        jnp.concatenate([expert_ids.astype(F32), gate_prob], axis=1), "tp", axis=0
+    )
+    chosen = both[:, :, :2].astype(jnp.int32).reshape(lanes, rows * 2)
+    hits = (chosen[:, :, None] == jnp.arange(EXPERTS, dtype=jnp.int32)).astype(jnp.int32)
+    earlier = jnp.cumsum(hits, axis=1) - hits
+    slot = jnp.sum(earlier * hits, axis=2)
+    source = jnp.arange(lanes, dtype=jnp.int32)[:, None]
+    target = (chosen * lanes + source) * capacity + slot
+    return target.reshape(lanes * rows, 2), both[:, :, 2:].reshape(lanes * rows, 2)
 
 
 def per_device(
@@ -298,6 +538,7 @@
     down_weight,
 ):
     tokens, channels = x_in.shape
+    route = routing(expert_ids, gate_prob)
     width = out_weight.shape[1]
     reach = conv_weight.shape[0] - 1
     rim_rows = shifted(x_in[tokens - reach :], "seq", 1)
@@ -319,56 +560,24 @@
         (ssm + skip_gain[None, :] * inner.astype(F32)) * jax.nn.silu(gate_in.astype(F32))
     ).astype(BF16)
     rows = tokens // lax.axis_size("tp")
-    mixer_out, normed_all = mixer_rows(
+    mixer_out, normed_part = mixer_rows(
         jnp.dot(mixed, out_weight, preferred_element_type=F32).astype(BF16), residual_in, norm_gain
     )
-    normed = lax.dynamic_index_in_dim(normed_all, lax.axis_index("tp"), 0, False)
-    mixer_wide = mixer_out.astype(F32)
-    seq_count = lax.axis_size("seq")
-    devices = seq_count * lax.axis_size("tp")
-    seq_group = seq_count // EXPERTS
+    count, lanes = lax.axis_size("seq"), lax.axis_size("tp")
+    group = count // EXPERTS
     capacity = 3 * rows // EXPERTS
-    chosen = expert_ids.reshape(-1)
-    expert_hits = (chosen[:, None] == jnp.arange(EXPERTS, dtype=jnp.int32)[None, :]).astype(
-        jnp.int32
-    )
-    earlier_hits = jnp.cumsum(expert_hits, axis=0) - expert_hits
-    slot_index = jnp.sum(earlier_hits * expert_hits, axis=1)
-    target = chosen * capacity + slot_index
-    placing = (jnp.arange(EXPERTS * capacity, dtype=jnp.int32)[:, None] == target[None, :]).astype(
-        jnp.bfloat16
-    )
-    placing = jnp.sum(placing.reshape(EXPERTS * capacity, rows, 2), axis=2)
-    slots_out = (
-        jnp.dot(placing, normed, preferred_element_type=jnp.float32)
-        .astype(jnp.bfloat16)
-        .reshape(EXPERTS, capacity, width)
-    )
-    along_seq = jnp.repeat(slots_out, seq_group, axis=0)
-    arrived_seq = lax.all_to_all(along_seq, "seq", split_axis=0, concat_axis=0, tiled=True)
-    arrived_all = lax.all_gather(
-        arrived_seq.reshape(1, seq_count * capacity, width), "tp", axis=0, tiled=True
-    )
-    arrived_flat = arrived_all.reshape(devices * capacity, width)
-    summed = lax.psum_scatter(
-        expert_share(arrived_flat, up_weight, down_weight).astype(jnp.float32).astype(jnp.bfloat16),
-        "tp",
-        scatter_dimension=0,
-        tiled=True,
-    ).astype(jnp.float32)
-    home = lax.all_to_all(
-        summed.reshape(seq_count, capacity, width).astype(jnp.bfloat16),
-        "seq",
-        split_axis=0,
-        concat_axis=0,
-        tiled=True,
-    ).astype(jnp.float32)
-    expert_out = jnp.sum(home.reshape(EXPERTS, seq_group, capacity, width), axis=1).reshape(
-        EXPERTS * capacity, width
-    )
-    picked = jnp.take(expert_out, target, axis=0).reshape(rows, 2, width)
-    layer_out = (mixer_wide + jnp.sum(picked * gate_prob[:, :, None], axis=1)).astype(jnp.bfloat16)
-    return (mixer_out, layer_out)
+    spread = lanes * capacity
+    target, prob = route
+    placing = jnp.sum(
+        (jnp.arange(EXPERTS * spread, dtype=jnp.int32)[:, None, None] == target[None]).astype(BF16),
+        axis=2,
+    )
+    column = jnp.arange(count * spread, dtype=jnp.int32)
+    column = column // (spread * group) * spread + column % spread
+    pick = (target.T.reshape(-1)[:, None] == column[None, :]).astype(BF16)
+    arrived = dispatch(placing, normed_part.reshape(tokens, width // lanes), group)
+    share = expert_share(arrived, up_weight, down_weight)
+    return (mixer_out, bring_back(share, pick, prob.T.reshape(-1, 1), mixer_out))
 
 
 def solution(mesh):

time: 276 us -> 188 us (0.68); the launches traced: 272 us -> 188 us
  waiting for transfers between devices: 89.1 us -> 0.01 us
  Pallas kernels: 53.2 us -> 124 us
  blocking collectives: 35.7 us -> 5.9 us
  between operations: 14.3 us -> 0.94 us
  local copies, waits for them, and re-layouts: 16.9 us -> 6.23 us
  starting transfers between devices: 8.89 us -> 3.15 us
  other arithmetic: 9.39 us -> 5.8 us
    pallas_call x0 -> x2, Pallas kernels: none -> 76 us  [the longest x1 40.1 us: bring_back(): pl.pallas_call(functools.partial(return_kernel, count, lanes), out_shape=...]
    reduce_scatter x1 -> x0, waiting for transfers between devices: 37.7 us -> none  [per_device(): lax.psum_scatter(expert_share(arrived_flat, up_weight, down_weight).astyp...]
    all_to_all x1 -> x0, blocking collectives: 35.7 us -> none  [per_device(): lax.all_to_all(along_seq, 'seq', split_axis=0, concat_axis=0, tiled=True)]
    all_gather x1 -> x0, waiting for transfers between devices: 29.8 us -> none  [per_device(): lax.all_gather(arrived_seq.reshape(1, seq_count * capacity, width), 'tp',...]
    all_to_all x1 -> x0, waiting for transfers between devices: 21.6 us -> none  [per_device(): lax.all_to_all(summed.reshape(seq_count, capacity, width).astype(jnp.bflo...]
    all_gather x0 -> x1, blocking collectives: none -> 5.9 us  [routing(): lax.all_gather(jnp.concatenate([expert_ids.astype(F32), gate_prob], axis=...]
    all_to_all x1 -> x0, starting transfers between devices: 5.48 us -> none  [per_device(): lax.all_to_all(summed.reshape(seq_count, capacity, width).astype(jnp.bflo...]
    pallas_call x1, Pallas kernels: 22.3 us -> 17.6 us  [mixer_rows(): pl.pallas_call(functools.partial(mixer_kernel, count), out_shape=(jax.Sha...]
  transfers between devices with their start and end apart: 4 -> 1, of which waited for: 3 -> 0; matrix products, arithmetic and copies ran while one was open for 2% -> 3% of each run, Pallas kernels for 0% -> 0%
where the time goes in v2:
time: 188 us
  Pallas kernels  124 us (66%)
  matrix products  42 us (22%)
  local copies, waits for them, and re-layouts  6.23 us (3%)
  blocking collectives  5.9 us (3%)
  other arithmetic  5.8 us (3%)
  starting transfers between devices  3.15 us (2%)
    pallas_call x1, Pallas kernels, bring_back(): pl.pallas_call(functools.partial(return_kernel, count, lanes), out_shape=...  40.1 us
    pallas_call x1, Pallas kernels, dispatch(): pl.pallas_call(functools.partial(dispatch_kernel, count, lanes, group), o...  35.9 us
    pallas_call x1, Pallas kernels, recur(): pl.pallas_call(functools.partial(scan_kernel, count), out_shape=jax.Shape...  21.1 us
    pallas_call x1, Pallas kernels, mixer_rows(): pl.pallas_call(functools.partial(mixer_kernel, count), out_shape=(jax.Sha...  17.6 us
    dot_general x1, matrix products, expert_share(): jnp.dot(arrived_flat, up_weight, preferred_element_type=F32)  15.2 us
    dot_general x1, matrix products, expert_share(): return jnp.dot(hidden, down_weight, preferred_element_type=F32).astype(BF16)  14.8 us
    pallas_call x1, Pallas kernels, sum_over_tp(): pl.pallas_call(functools.partial(sum_kernel, count), out_shape=jax.ShapeD...  9.01 us
    dot_general x1, matrix products, per_device(): jnp.dot(mixed, out_weight, preferred_element_type=F32).astype(BF16)  8.58 us
  transfers between devices with their start and end apart: 1, of which 0 were waited for; matrix products, arithmetic and copies ran while one was open for 3% of the time, Pallas kernels for 0%

profile of v2, /device:TPU:13, one launch (start us, length us, event | category | flops | bytes accessed | tf_op | source)
XLA Modules:
  0.0 187.7 jit_solution(17817411207697738418)
XLA Ops:
  0.6 0.0 copy-start
  0.6 0.0 copy-start.5
  0.7 0.9 slice.41
  1.6 3.1 %collective-permute-start = (bf16[3,2048]{1,0:T(4,128)(2,1)S(1)}, bf16[3,2048]{1,0:T(4,128)(2,1)S(1)}, u32[]{:S(2)}, u32[]{:S(2)}) collective-permute-start(bf16[3,2048]{1,0:T(4,128)(2,1)S(1)} %slice.41), channel_id=1, source_target_pairs={{0,4},{4,8},{8,12},{12,16},{16,20},{20,24},{24,28},{1,5},{5,9},{9,... | collective-permute-start | bytes 36872 | tf_op jit(solution)/shard_map/ppermute | solution.py:24
  4.7 0.7 convert_element_type.53
  5.4 0.7 maximum_bitcast_fusion
  6.1 5.9 %all-gather.1 = f32[4,32,4]{1,2,0:T(4,128)S(1)} all-gather(f32[1,32,4]{1,2,0:T(4,128)S(1)} %maximum_bitcast_fusion), channel_id=2, replica_groups=mesh['seq'=8,'tp'=4] {'tp'}, dimensions={0}, use_global_device_ids=true | all-gather | bytes 2560 | tf_op jit(solution)/shard_map/all_gather | solution.py:510
  12.1 0.9 fusion.29
  13.0 0.9 negate_bitcast_fusion
  13.9 0.1 copy.47
  14.0 0.1 copy.48
  14.1 0.1 fusion.17
  14.2 0.1 reduce_window_sum.11
  14.4 0.2 select_reduce_fusion
  14.6 0.1 reduce_sum.24
  14.7 0.1 copy.49
  14.8 0.1 mul.119
  14.8 0.1 add.112
  14.9 0.1 add.118
  15.1 0.1 compare_convert_fusion.pick_ref
  15.3 0.1 reshape.89
  15.4 0.1 copy.52.prob_ref
  15.5 0.0 collective-permute-done
  15.5 1.2 maximum_convert_fusion
  16.7 1.6 convert_bitcast_fusion
  18.4 0.0 copy-done
  18.4 0.8 convolution_convert_fusion.2
  19.1 0.8 copy.45.part_ref
  19.9 9.0 %projection_sum.1 = f32[128,544]{1,0:T(8,128)} custom-call(bf16[128,544]{1,0:T(8,128)(2,1)} %copy.45.part_ref), custom_call_target="tpu_custom_call" | custom-call | tf_op jit(solution)/shard_map/projection_sum/pallas_call | solution.py:78
  29.0 0.8 slice.50.maps_ref
  29.8 0.0 copy-done.7
  29.8 2.6 %fusion.7 = f32[16,8,16,128]{3,1,2,0:T(8,128)S(1)} fusion(bf16[512,2048]{1,0:T(8,128)(2,1)} %param.21, f32[2048]{0:T(1024)S(1)} %copy-done.7, f32[128,544]{1,0:T(8,128)} %projection_sum.1), kind=kOutput, calls=%fused_computation.17 | convolution fusion | flops 270270464 | bytes 3284992 | tf_op jit(solution)/shard_map/dot_general | solution.py:556
  32.5 0.2 copy.54
  32.7 0.0 copy-start.6
  32.7 0.0 copy-start.8
  32.7 0.2 copy.55
  32.9 21.1 %recurrence.1 = f32[128,16,128]{2,1,0:T(8,128)S(1)} custom-call(f32[128,16,128]{2,1,0:T(8,128)S(1)} %bitcast.50, f32[128,16,128]{2,1,0:T(8,128)S(1)} %bitcast.51, f32[128,32]{1,0:T(8,128)S(1)} %slice.50.maps_ref, f32[16,16,128]{2,1,0:T(8,128)S(1)} %bitcast.54), custom_call_target="tpu_custom_call" | custom-call | tf_op jit(solution)/shard_map/recurrence/pallas_call | solution.py:178
  54.0 0.0 copy-start.2
  54.0 0.0 copy-start.3
  54.1 8.6 %convolution_convert_fusion.1 = bf16[128,4096]{1,0:T(8,128)(2,1)S(1)} fusion(bf16[2048,4096]{1,0:T(8,128)(2,1)} %param.25, bf16[128,2048]{1,0:T(8,128)(2,1)S(1)} %get-tuple-element.7, bf16[128,2048]{1,0:T(8,128)(2,1)S(1)} %copy-done.6, f32[16,8,16,128]{3,2,1,0:T(8,128)S(1)} %bitcast.52, f32[2048]{0:T(1024)S(1)} %copy-done.8), kind=kOutput, calls=%fused_computation.1 | convolution fusion | flops 2150629376 | bytes 19931136 | tf_op jit(solution)/shard_map/dot_general | solution.py:564
  62.7 17.6 %mixer_sum.1 = (bf16[32,4096]{1,0:T(8,128)(2,1)S(1)}, bf16[4,32,1024]{2,1,0:T(8,128)(2,1)S(1)}) custom-call(bf16[4,32,4096]{2,1,0:T(8,128)(2,1)S(1)} %bitcast.53, bf16[32,4096]{1,0:T(8,128)(2,1)S(1)} %copy-done.2, f32[1,4096]{1,0:T(1,128)S(1)} %bitcast.56), custom_call_target="tpu_custom_call" | custom-call | tf_op jit(solution)/shard_map/mixer_sum/pallas_call | solution.py:259
  80.3 35.9 %dispatch.1 = bf16[384,4096]{1,0:T(8,128)(2,1)S(1)} custom-call(bf16[384,128]{1,0:T(8,128)(2,1)S(1)} %fusion.16.placing_ref, bf16[128,1024]{1,0:T(8,128)(2,1)S(1)} %bitcast.55), custom_call_target="tpu_custom_call" | custom-call | tf_op jit(solution)/shard_map/dispatch/pallas_call | solution.py:364
  116.1 15.2 %multiply_convert_fusion.6 = bf16[384,3072]{1,0:T(8,128)(2,1)S(1)} fusion(bf16[384,4096]{1,0:T(8,128)(2,1)S(1)} %dispatch.1, bf16[4096,3072]{1,0:T(8,128)(2,1)} %param.30), kind=kOutput, calls=%fused_computation.2.clone.clone.1 | convolution fusion | flops 9669574656 | bytes 30670848 | tf_op jit(solution)/shard_map/dot_general | solution.py:502
  131.3 0.0 copy-start.1
  131.3 14.8 %convolution_convert_fusion.part_ref = bf16[384,4096]{1,0:T(8,128)(2,1)S(1)} fusion(bf16[3072,4096]{1,0:T(8,128)(2,1)} %param.31, bf16[384,3072]{1,0:T(8,128)(2,1)S(1)} %multiply_convert_fusion.6), kind=kOutput, calls=%fused_computation | convolution fusion | flops 9665249280 | bytes 30670848 | tf_op jit(solution)/shard_map/dot_general | solution.py:503
  146.2 40.1 %bring_back.1 = bf16[32,4096]{1,0:T(8,128)(2,1)S(1)} custom-call(bf16[384,4096]{1,0:T(8,128)(2,1)S(1)} %convolution_convert_fusion.part_ref, bf16[256,384]{1,0:T(8,128)(2,1)S(1)} %compare_convert_fusion.pick_ref, f32[256,1]{1,0:T(8,128)S(1)} %copy.52.prob_ref, bf16[32,4096]{1,0:T(8,128)(2,1)S(1)} %get-tuple-element.18.mixer_ref), custom_call_target="tpu_custom_call" | custom-call | tf_op jit(solution)/shard_map/bring_back/pallas_call | solution.py:483
  186.3 0.7 copy.65
  187.0 0.7 copy.66
  (19 shorter events, 0.1 us)
Async XLA Ops:
  0.6 17.7 %copy-start = (bf16[2048,544]{0,1:T(8,128)(2,1)S(1)}, bf16[2048,544]{0,1:T(8,128)(2,1)}, u32[]{:S(2)}) copy-start(bf16[2048,544]{0,1:T(8,128)(2,1)} %param.20) | copy-start | bytes 6684676
  0.6 16.1 %copy-start.5 = (f32[2048]{0:T(1024)S(1)}, f32[2048]{0:T(1024)}, u32[]{:S(2)}) copy-start(f32[2048]{0:T(1024)} %param.19) | copy-start | bytes 24580
  1.6 13.9 %collective-permute-start = (bf16[3,2048]{1,0:T(4,128)(2,1)S(1)}, bf16[3,2048]{1,0:T(4,128)(2,1)S(1)}, u32[]{:S(2)}, u32[]{:S(2)}) collective-permute-start(bf16[3,2048]{1,0:T(4,128)(2,1)S(1)} %slice.41), channel_id=1, source_target_pairs={{0,4},{4,8},{8,12},{12,16},{16,20},{20,24},{24,28},{1,5},{5,9},{9,... | collective-permute-start | bytes 36872 | tf_op jit(solution)/shard_map/ppermute | solution.py:24
  18.4 11.4 %copy-start.7 = (f32[2048]{0:T(1024)S(1)}, f32[2048]{0:T(1024)}, u32[]{:S(2)}) copy-start(f32[2048]{0:T(1024)} %param.22) | copy-start | bytes 24580
  29.8 2.9 %copy-start.4 = (f32[16,8,16,128]{3,1,2,0:T(8,128)S(1)}, f32[16,8,16,128]{3,1,2,0:T(8,128)}, u32[]{:S(2)}) copy-start(f32[16,8,16,128]{3,1,2,0:T(8,128)} %get-tuple-element.6) | copy-start | bytes 3145732
  32.7 21.4 %copy-start.6 = (bf16[128,2048]{1,0:T(8,128)(2,1)S(1)}, bf16[128,2048]{1,0:T(8,128)(2,1)}, u32[]{:S(2)}) copy-start(bf16[128,2048]{1,0:T(8,128)(2,1)} %param.17) | copy-start | bytes 1572868
  32.7 21.4 %copy-start.8 = (f32[2048]{0:T(1024)S(1)}, f32[2048]{0:T(1024)}, u32[]{:S(2)}) copy-start(f32[2048]{0:T(1024)} %param.24) | copy-start | bytes 24580
  54.0 8.6 %copy-start.2 = (bf16[32,4096]{1,0:T(8,128)(2,1)S(1)}, bf16[32,4096]{1,0:T(8,128)(2,1)}, u32[]{:S(2)}) copy-start(bf16[32,4096]{1,0:T(8,128)(2,1)} %residual_ref.1) | copy-start | bytes 786436
  54.0 8.6 %copy-start.3 = (f32[4096]{0:T(1024)S(1)}, f32[4096]{0:T(1024)}, u32[]{:S(2)}) copy-start(f32[4096]{0:T(1024)} %param.27) | copy-start | bytes 49156
  131.3 56.4 %copy-start.1 = (bf16[2048,544]{0,1:T(8,128)(2,1)S(1)}, bf16[2048,544]{0,1:T(8,128)(2,1)}, u32[]{:S(2)}) copy-start(bf16[2048,544]{0,1:T(8,128)(2,1)} %param.20) | copy-start | bytes 6684676

commit v3 on v2

--- a/solution.py
+++ b/solution.py
@@ -16,6 +16,8 @@
 F32 = jnp.float32
 BF16 = jnp.bfloat16
 MIB = 1024 * 1024
+AHEAD = 3
+LAG = 2
 
 
 def shifted(value, axis, steps):
@@ -54,41 +56,74 @@
     return count.bit_length() - 1
 
 
-def sum_kernel(count, part_ref, out_ref, outgoing, arriving, send_sems, recv_sems):
+def sum_kernel(
+    count,
+    part_ref,
+    route_ref,
+    out_ref,
+    routes_ref,
+    outgoing,
+    arriving,
+    send_sems,
+    recv_sems,
+    route_send_sems,
+    route_recv_sems,
+):
     me = lax.axis_index("tp")
     stages = stages_of(count)
-    greet([{"tp": flipped(me, k)} for k in range(stages)])
+    greet([{"tp": lax.rem(me + d, count)} for d in range(1, count)])
+    routes = [
+        send(
+            route_ref,
+            routes_ref.at[me],
+            route_send_sems.at[d],
+            route_recv_sems.at[d],
+            {"tp": lax.rem(me + d, count)},
+        )
+        for d in range(1, count)
+    ]
     for k in range(stages):
         source = part_ref if k == 0 else outgoing
         copy = send(
             source, arriving.at[k], send_sems.at[k], recv_sems.at[k], {"tp": flipped(me, k)}
         )
         copy.start()
+        if k == 0:
+            for route in routes:
+                route.start()
+            routes_ref[me] = route_ref[...]
         copy.wait()
         total = source[...].astype(F32) + arriving[k].astype(F32)
         if k < stages - 1:
             outgoing[...] = total.astype(BF16)
         else:
             out_ref[...] = total
-
-
-def sum_over_tp(part):
+    for route in routes:
+        route.wait()
+
+
+def sum_over_tp(part, route):
     count = lax.axis_size("tp")
     stages = stages_of(count)
     return pl.pallas_call(
         functools.partial(sum_kernel, count),
-        out_shape=jax.ShapeDtypeStruct(part.shape, F32),
-        in_specs=[VMEM_SPEC],
-        out_specs=VMEM_SPEC,
+        out_shape=(
+            jax.ShapeDtypeStruct(part.shape, F32),
+            jax.ShapeDtypeStruct((count, *route.shape), F32),
+        ),
+        in_specs=[VMEM_SPEC] * 2,
+        out_specs=(VMEM_SPEC, VMEM_SPEC),
         scratch_shapes=[
             pltpu.VMEM(part.shape, BF16),
             pltpu.VMEM((stages, *part.shape), BF16),
             pltpu.SemaphoreType.DMA((stages,)),
             pltpu.SemaphoreType.DMA((stages,)),
+            pltpu.SemaphoreType.DMA((count,)),
+            pltpu.SemaphoreType.DMA((count,)),
         ],
         compiler_params=pltpu.CompilerParams(collective_id=0, has_side_effects=True),
         name="projection_sum",
-    )(part)
+    )(part, route)
 
 
 def scan_kernel(
@@ -318,18 +353,21 @@
                 {"seq": target},
             )
         )
-        firsts[-1].start()
+        if d <= AHEAD:
+            firsts[-1].start()
     out_ref[block(me, lane)] = slots[me // group]
 
     spread = {}
-    for step in range(count + stages - 1):
+    for step in range(count + LAG * (stages - 1)):
         for k in range(stages - 1, -1, -1):
-            d = step - (stages - 1 - k)
+            d = step - LAG * (stages - 1 - k)
             if d < 0 or d >= count:
                 continue
             if k == stages - 1:
                 if d > 0:
                     firsts[d - 1].wait_recv()
+                    if d + AHEAD < count:
+                        firsts[d - 1 + AHEAD].start()
             else:
                 for copy in spread[d, k + 1]:
                     copy.wait_recv()
@@ -425,11 +463,11 @@
     order = list(range(1, count)) + [0]
     sums = {(d, 0): start(d, 0) for d in order}
     homes = []
-    for step in range(count + stages - 1):
+    for step in range(count + LAG * (stages - 1)):
         for k in range(stages):
-            if step - k < 0 or step - k >= count:
+            if step - LAG * k < 0 or step - LAG * k >= count:
                 continue
-            d = order[step - k]
+            d = order[step - LAG * k]
             finish(d, k, sums[d, k])
             if k < stages - 1:
                 sums[d, k + 1] = start(d, k + 1)
@@ -503,13 +541,9 @@
     return jnp.dot(hidden, down_weight, preferred_element_type=F32).astype(BF16)
 
 
-def routing(expert_ids, gate_prob):
-    rows = expert_ids.shape[0]
-    lanes = lax.axis_size("tp")
+def routing(both):
+    lanes, rows = both.shape[:2]
     capacity = 3 * rows // EXPERTS
-    both = lax.all_gather(
-        jnp.concatenate([expert_ids.astype(F32), gate_prob], axis=1), "tp", axis=0
-    )
     chosen = both[:, :, :2].astype(jnp.int32).reshape(lanes, rows * 2)
     hits = (chosen[:, :, None] == jnp.arange(EXPERTS, dtype=jnp.int32)).astype(jnp.int32)
     earlier = jnp.cumsum(hits, axis=1) - hits
@@ -538,7 +572,6 @@
     down_weight,
 ):
     tokens, channels = x_in.shape
-    route = routing(expert_ids, gate_prob)
     width = out_weight.shape[1]
     reach = conv_weight.shape[0] - 1
     rim_rows = shifted(x_in[tokens - reach :], "seq", 1)
@@ -550,7 +583,10 @@
         )
     )
     inner = jax.nn.silu(conv_out).astype(BF16)
-    projected = sum_over_tp(jnp.dot(inner, x_weight, preferred_element_type=F32).astype(BF16))
+    projected, both = sum_over_tp(
+        jnp.dot(inner, x_weight, preferred_element_type=F32).astype(BF16),
+        jnp.concatenate([expert_ids.astype(F32), gate_prob], axis=1),
+    )
     dt_low = projected[:, :DTRANK].astype(BF16)
     step_size = jax.nn.softplus(
         jnp.dot(dt_low, dt_weight, preferred_element_type=F32) + dt_bias[None, :]
@@ -567,7 +603,7 @@
     group = count // EXPERTS
     capacity = 3 * rows // EXPERTS
     spread = lanes * capacity
-    target, prob = route
+    target, prob = routing(both)
     placing = jnp.sum(
         (jnp.arange(EXPERTS * spread, dtype=jnp.int32)[:, None, None] == target[None]).astype(BF16),
         axis=2,

time: 188 us -> 186 us (0.989)
  blocking collectives: 5.9 us -> 0 us
  other arithmetic: 5.8 us -> 8.43 us
    all_gather x1 -> x0, blocking collectives: 5.9 us -> none  [routing(): lax.all_gather(jnp.concatenate([expert_ids.astype(F32), gate_prob], axis=...]
  transfers between devices with their start and end apart: 1 -> 1, of which waited for: 0 -> 0; matrix products, arithmetic and copies ran while one was open for 3% -> 2% of each run, Pallas kernels for 0% -> 0%
where the time goes in v3:
time: 186 us
  Pallas kernels  124 us (67%)
  matrix products  42.1 us (23%)
  other arithmetic  8.43 us (5%)
  local copies, waits for them, and re-layouts  7.11 us (4%)
  starting transfers between devices  3.15 us (2%)
    pallas_call x1, Pallas kernels, bring_back(): pl.pallas_call(functools.partial(return_kernel, count, lanes), out_shape=...  39.7 us
    pallas_call x1, Pallas kernels, dispatch(): pl.pallas_call(functools.partial(dispatch_kernel, count, lanes, group), o...  35.9 us
    pallas_call x1, Pallas kernels, recur(): pl.pallas_call(functools.partial(scan_kernel, count), out_shape=jax.Shape...  21.1 us
    pallas_call x1, Pallas kernels, mixer_rows(): pl.pallas_call(functools.partial(mixer_kernel, count), out_shape=(jax.Sha...  17.6 us
    dot_general x1, matrix products, expert_share(): jnp.dot(arrived_flat, up_weight, preferred_element_type=F32)  15.3 us
    dot_general x1, matrix products, expert_share(): return jnp.dot(hidden, down_weight, preferred_element_type=F32).astype(BF16)  14.9 us
    pallas_call x1, Pallas kernels, sum_over_tp(): pl.pallas_call(functools.partial(sum_kernel, count), out_shape=(jax.Shape...  9.88 us
    dot_general x1, matrix products, per_device(): jnp.dot(mixed, out_weight, preferred_element_type=F32).astype(BF16)  8.53 us
  transfers between devices with their start and end apart: 1, of which 0 were waited for; matrix products, arithmetic and copies ran while one was open for 2% of the time, Pallas kernels for 0%

profile of v3, /device:TPU:13, one launch (start us, length us, event | category | flops | bytes accessed | tf_op | source)
XLA Modules:
  0.0 185.8 jit_solution(3796327648935179338)
XLA Ops:
  0.6 0.0 copy-start
  0.6 0.9 slice.41
  1.6 3.1 %collective-permute-start = (bf16[3,2048]{1,0:T(4,128)(2,1)S(1)}, bf16[3,2048]{1,0:T(4,128)(2,1)S(1)}, u32[]{:S(2)}, u32[]{:S(2)}) collective-permute-start(bf16[3,2048]{1,0:T(4,128)(2,1)S(1)} %slice.41), channel_id=1, source_target_pairs={{0,4},{4,8},{8,12},{12,16},{16,20},{20,24},{24,28},{1,5},{5,9},{9,... | collective-permute-start | bytes 36872 | tf_op jit(solution)/shard_map/ppermute | solution.py:26
  4.7 0.9 fusion.34
  5.7 0.7 convert_element_type.49
  6.4 0.9 negate_bitcast_fusion
  7.3 0.7 pad_maximum_fusion
  8.0 0.7 copy.46.route_ref
  8.7 0.1 add.112
  8.8 0.1 add.118
  8.9 1.2 maximum_convert_fusion
  10.1 2.3 %convert_bitcast_fusion = (f32[16,8,16,128]{3,1,2,0:T(8,128)}, bf16[128,2048]{1,0:T(8,128)(2,1)S(1)}) fusion(f32[131,2048]{1,0:T(8,128)S(1)} %maximum_convert_fusion, f32[2048]{0:T(1024)S(1)} %bitcast.66, f32[2048]{0:T(1024)S(1)} %bitcast.67, f32[2048]{0:T(1024)S(1)} %bitcast.65, f32[2048]{0:T(1024)S(1)} %bitcast.64, f32[2048]{0:T(1024)} %param.19), kind=kLoop, calls=%fused_computation.9 | loop fusion | flops 3670016 | bytes 5808128
  12.4 0.7 convolution_convert_fusion.2
  13.2 0.8 copy.45.part_ref
  14.0 9.9 %projection_sum.1 = (f32[128,544]{1,0:T(8,128)}, f32[4,32,4]{2,1,0:T(8,128)}) custom-call(bf16[128,544]{1,0:T(8,128)(2,1)} %copy.45.part_ref, f32[32,4]{1,0:T(8,128)} %copy.46.route_ref), custom_call_target="tpu_custom_call" | custom-call | tf_op jit(solution)/shard_map/projection_sum/pallas_call | solution.py:108
  23.9 1.0 fusion.33
  24.9 0.9 broadcast_multiply_fusion
  25.7 0.8 slice.50.maps_ref
  26.6 2.6 %fusion.7 = f32[16,8,16,128]{3,1,2,0:T(8,128)S(1)} fusion(bf16[512,2048]{1,0:T(8,128)(2,1)} %param.21, f32[2048]{0:T(1024)S(1)} %copy-done.6, f32[128,544]{1,0:T(8,128)} %get-tuple-element.6), kind=kOutput, calls=%fused_computation.17 | convolution fusion | flops 270270464 | bytes 3284992 | tf_op jit(solution)/shard_map/dot_general | solution.py:592
  29.3 0.2 copy.53
  29.5 0.0 copy-start.7
  29.5 0.2 copy.54
  29.7 0.3 copy.47
  30.0 0.1 copy.48
  30.1 0.1 fusion.17
  30.2 0.1 reduce_window_sum.11
  30.3 0.2 select_reduce_fusion
  30.5 0.1 reduce_sum.24
  30.7 0.1 fusion.21
  30.8 0.1 copy.49
  30.8 0.1 fusion.16.placing_ref
  30.9 0.1 copy.50
  31.0 0.1 copy.51
  31.0 0.2 copy.52.prob_ref
  31.2 0.0 copy-start.5
  31.2 21.1 %recurrence.1 = f32[128,16,128]{2,1,0:T(8,128)S(1)} custom-call(f32[128,16,128]{2,1,0:T(8,128)S(1)} %bitcast.54, f32[128,16,128]{2,1,0:T(8,128)S(1)} %bitcast.55, f32[128,32]{1,0:T(8,128)S(1)} %slice.50.maps_ref, f32[16,16,128]{2,1,0:T(8,128)S(1)} %bitcast.58), custom_call_target="tpu_custom_call" | custom-call | tf_op jit(solution)/shard_map/recurrence/pallas_call | solution.py:213
  52.4 0.0 copy-start.2
  52.4 0.0 copy-start.3
  52.4 8.5 %convolution_convert_fusion.1 = bf16[128,4096]{1,0:T(8,128)(2,1)S(1)} fusion(bf16[2048,4096]{1,0:T(8,128)(2,1)} %param.25, bf16[128,2048]{1,0:T(8,128)(2,1)S(1)} %get-tuple-element.11, bf16[128,2048]{1,0:T(8,128)(2,1)S(1)} %copy-done.5, f32[16,8,16,128]{3,2,1,0:T(8,128)S(1)} %bitcast.56, f32[2048]{0:T(1024)S(1)} %copy-done.7), kind=kOutput, calls=%fused_computation.1 | convolution fusion | flops 2150629376 | bytes 19931136 | tf_op jit(solution)/shard_map/dot_general | solution.py:600
  61.0 17.6 %mixer_sum.1 = (bf16[32,4096]{1,0:T(8,128)(2,1)S(1)}, bf16[4,32,1024]{2,1,0:T(8,128)(2,1)S(1)}) custom-call(bf16[4,32,4096]{2,1,0:T(8,128)(2,1)S(1)} %bitcast.57, bf16[32,4096]{1,0:T(8,128)(2,1)S(1)} %copy-done.2, f32[1,4096]{1,0:T(1,128)S(1)} %bitcast.60), custom_call_target="tpu_custom_call" | custom-call | tf_op jit(solution)/shard_map/mixer_sum/pallas_call | solution.py:294
  78.5 35.9 %dispatch.1 = bf16[384,4096]{1,0:T(8,128)(2,1)S(1)} custom-call(bf16[384,128]{1,0:T(8,128)(2,1)S(1)} %fusion.16.placing_ref, bf16[128,1024]{1,0:T(8,128)(2,1)S(1)} %bitcast.59), custom_call_target="tpu_custom_call" | custom-call | tf_op jit(solution)/shard_map/dispatch/pallas_call | solution.py:402
  114.4 15.3 %multiply_convert_fusion.6 = bf16[384,3072]{1,0:T(8,128)(2,1)S(1)} fusion(bf16[384,4096]{1,0:T(8,128)(2,1)S(1)} %dispatch.1, bf16[4096,3072]{1,0:T(8,128)(2,1)} %param.30), kind=kOutput, calls=%fused_computation.2.clone.clone.1 | convolution fusion | flops 9669574656 | bytes 30670848 | tf_op jit(solution)/shard_map/dot_general | solution.py:540
  129.7 0.0 copy-start.1
  129.7 14.9 %convolution_convert_fusion.part_ref = bf16[384,4096]{1,0:T(8,128)(2,1)S(1)} fusion(bf16[3072,4096]{1,0:T(8,128)(2,1)} %param.31, bf16[384,3072]{1,0:T(8,128)(2,1)S(1)} %multiply_convert_fusion.6), kind=kOutput, calls=%fused_computation | convolution fusion | flops 9665249280 | bytes 30670848 | tf_op jit(solution)/shard_map/dot_general | solution.py:541
  144.6 0.1 compare_convert_fusion.pick_ref
  144.7 39.7 %bring_back.1 = bf16[32,4096]{1,0:T(8,128)(2,1)S(1)} custom-call(bf16[384,4096]{1,0:T(8,128)(2,1)S(1)} %convolution_convert_fusion.part_ref, bf16[256,384]{1,0:T(8,128)(2,1)S(1)} %compare_convert_fusion.pick_ref, f32[256,1]{1,0:T(8,128)S(1)} %copy.52.prob_ref, bf16[32,4096]{1,0:T(8,128)(2,1)S(1)} %get-tuple-element.22.mixer_ref), custom_call_target="tpu_custom_call" | custom-call | tf_op jit(solution)/shard_map/bring_back/pallas_call | solution.py:521
  184.4 0.7 copy.61
  185.1 0.7 copy.62
  (15 shorter events, 0.1 us)
Async XLA Ops:
  0.6 11.8 %copy-start = (bf16[2048,544]{0,1:T(8,128)(2,1)S(1)}, bf16[2048,544]{0,1:T(8,128)(2,1)}, u32[]{:S(2)}) copy-start(bf16[2048,544]{0,1:T(8,128)(2,1)} %param.20) | copy-start | bytes 6684676
  1.6 7.3 %collective-permute-start = (bf16[3,2048]{1,0:T(4,128)(2,1)S(1)}, bf16[3,2048]{1,0:T(4,128)(2,1)S(1)}, u32[]{:S(2)}, u32[]{:S(2)}) collective-permute-start(bf16[3,2048]{1,0:T(4,128)(2,1)S(1)} %slice.41), channel_id=1, source_target_pairs={{0,4},{4,8},{8,12},{12,16},{16,20},{20,24},{24,28},{1,5},{5,9},{9,... | collective-permute-start | bytes 36872 | tf_op jit(solution)/shard_map/ppermute | solution.py:26
  12.4 14.2 %copy-start.6 = (f32[2048]{0:T(1024)S(1)}, f32[2048]{0:T(1024)}, u32[]{:S(2)}) copy-start(f32[2048]{0:T(1024)} %param.22) | copy-start | bytes 24580
  26.6 2.9 %copy-start.4 = (f32[16,8,16,128]{3,1,2,0:T(8,128)S(1)}, f32[16,8,16,128]{3,1,2,0:T(8,128)}, u32[]{:S(2)}) copy-start(f32[16,8,16,128]{3,1,2,0:T(8,128)} %get-tuple-element.10) | copy-start | bytes 3145732
  29.5 22.9 %copy-start.7 = (f32[2048]{0:T(1024)S(1)}, f32[2048]{0:T(1024)}, u32[]{:S(2)}) copy-start(f32[2048]{0:T(1024)} %param.24) | copy-start | bytes 24580
  31.2 21.1 %copy-start.5 = (bf16[128,2048]{1,0:T(8,128)(2,1)S(1)}, bf16[128,2048]{1,0:T(8,128)(2,1)}, u32[]{:S(2)}) copy-start(bf16[128,2048]{1,0:T(8,128)(2,1)} %param.17) | copy-start | bytes 1572868
  52.4 8.6 %copy-start.2 = (bf16[32,4096]{1,0:T(8,128)(2,1)S(1)}, bf16[32,4096]{1,0:T(8,128)(2,1)}, u32[]{:S(2)}) copy-start(bf16[32,4096]{1,0:T(8,128)(2,1)} %residual_ref.1) | copy-start | bytes 786436
  52.4 8.6 %copy-start.3 = (f32[4096]{0:T(1024)S(1)}, f32[4096]{0:T(1024)}, u32[]{:S(2)}) copy-start(f32[4096]{0:T(1024)} %param.27) | copy-start | bytes 49156
  129.7 56.1 %copy-start.1 = (bf16[2048,544]{0,1:T(8,128)(2,1)S(1)}, bf16[2048,544]{0,1:T(8,128)(2,1)}, u32[]{:S(2)}) copy-start(bf16[2048,544]{0,1:T(8,128)(2,1)} %param.20) | copy-start | bytes 6684676

commit v4 on v3

--- a/solution.py
+++ b/solution.py
@@ -157,7 +157,7 @@
         return states, total + step
 
     zero = jnp.zeros(tile, F32)
-    states, total = lax.fori_loop(0, tokens, ending, ((zero,) * STATE, zero))
+    states, total = lax.fori_loop(0, tokens, ending, ((zero,) * STATE, zero), unroll=4)
     for n in range(STATE):
         outgoing[n] = states[n].astype(BF16)
     upper = total.astype(BF16)
@@ -197,7 +197,7 @@
         out_ref[t] = terms[0]
         return states
 
-    lax.fori_loop(0, tokens, reading, tuple(state[n] for n in range(STATE)))
+    lax.fori_loop(0, tokens, reading, tuple(state[n] for n in range(STATE)), unroll=4)
     for d in range(1, count):
 
         @pl.when(me + d < count)

time: 186 us -> 184 us (0.989)
  Pallas kernels: 124 us -> 122 us
where the time goes in v4:
time: 184 us
  Pallas kernels  122 us (66%)
  matrix products  42.1 us (23%)
  other arithmetic  8.43 us (5%)
  local copies, waits for them, and re-layouts  7.11 us (4%)
  starting transfers between devices  3.15 us (2%)
    pallas_call x1, Pallas kernels, bring_back(): pl.pallas_call(functools.partial(return_kernel, count, lanes), out_shape=...  39.7 us
    pallas_call x1, Pallas kernels, dispatch(): pl.pallas_call(functools.partial(dispatch_kernel, count, lanes, group), o...  35.6 us
    pallas_call x1, Pallas kernels, recur(): pl.pallas_call(functools.partial(scan_kernel, count), out_shape=jax.Shape...  20 us
    pallas_call x1, Pallas kernels, mixer_rows(): pl.pallas_call(functools.partial(mixer_kernel, count), out_shape=(jax.Sha...  16.8 us
    dot_general x1, matrix products, expert_share(): jnp.dot(arrived_flat, up_weight, preferred_element_type=F32)  15.3 us
    dot_general x1, matrix products, expert_share(): return jnp.dot(hidden, down_weight, preferred_element_type=F32).astype(BF16)  14.9 us
    pallas_call x1, Pallas kernels, sum_over_tp(): pl.pallas_call(functools.partial(sum_kernel, count), out_shape=(jax.Shape...  9.88 us
    dot_general x1, matrix products, per_device(): jnp.dot(mixed, out_weight, preferred_element_type=F32).astype(BF16)  8.53 us
  transfers between devices with their start and end apart: 1, of which 0 were waited for; matrix products, arithmetic and copies ran while one was open for 2% of the time, Pallas kernels for 0%

profile of v4, /device:TPU:13, one launch (start us, length us, event | category | flops | bytes accessed | tf_op | source)
XLA Modules:
  0.0 183.7 jit_solution(7411683785210879758)
XLA Ops:
  0.6 0.0 copy-start
  0.6 0.9 slice.41
  1.6 3.1 %collective-permute-start = (bf16[3,2048]{1,0:T(4,128)(2,1)S(1)}, bf16[3,2048]{1,0:T(4,128)(2,1)S(1)}, u32[]{:S(2)}, u32[]{:S(2)}) collective-permute-start(bf16[3,2048]{1,0:T(4,128)(2,1)S(1)} %slice.41), channel_id=1, source_target_pairs={{0,4},{4,8},{8,12},{12,16},{16,20},{20,24},{24,28},{1,5},{5,9},{9,... | collective-permute-start | bytes 36872 | tf_op jit(solution)/shard_map/ppermute | solution.py:26
  4.7 0.9 fusion.34
  5.7 0.7 convert_element_type.49
  6.4 0.9 negate_bitcast_fusion
  7.3 0.7 pad_maximum_fusion
  8.0 0.7 copy.46.route_ref
  8.7 0.1 add.112
  8.8 0.1 add.118
  8.9 1.2 maximum_convert_fusion
  10.1 2.3 %convert_bitcast_fusion = (f32[16,8,16,128]{3,1,2,0:T(8,128)}, bf16[128,2048]{1,0:T(8,128)(2,1)S(1)}) fusion(f32[131,2048]{1,0:T(8,128)S(1)} %maximum_convert_fusion, f32[2048]{0:T(1024)S(1)} %bitcast.66, f32[2048]{0:T(1024)S(1)} %bitcast.67, f32[2048]{0:T(1024)S(1)} %bitcast.65, f32[2048]{0:T(1024)S(1)} %bitcast.64, f32[2048]{0:T(1024)} %param.19), kind=kLoop, calls=%fused_computation.9 | loop fusion | flops 3670016 | bytes 5808128
  12.4 0.7 convolution_convert_fusion.2
  13.2 0.8 copy.45.part_ref
  14.0 9.9 %projection_sum.1 = (f32[128,544]{1,0:T(8,128)}, f32[4,32,4]{2,1,0:T(8,128)}) custom-call(bf16[128,544]{1,0:T(8,128)(2,1)} %copy.45.part_ref, f32[32,4]{1,0:T(8,128)} %copy.46.route_ref), custom_call_target="tpu_custom_call" | custom-call | tf_op jit(solution)/shard_map/projection_sum/pallas_call | solution.py:108
  23.9 1.0 fusion.33
  24.9 0.9 broadcast_multiply_fusion
  25.7 0.8 slice.50.maps_ref
  26.6 2.6 %fusion.7 = f32[16,8,16,128]{3,1,2,0:T(8,128)S(1)} fusion(bf16[512,2048]{1,0:T(8,128)(2,1)} %param.21, f32[2048]{0:T(1024)S(1)} %copy-done.6, f32[128,544]{1,0:T(8,128)} %get-tuple-element.6), kind=kOutput, calls=%fused_computation.17 | convolution fusion | flops 270270464 | bytes 3284992 | tf_op jit(solution)/shard_map/dot_general | solution.py:592
  29.3 0.2 copy.53
  29.5 0.0 copy-start.7
  29.5 0.2 copy.54
  29.7 0.3 copy.47
  30.0 0.1 copy.48
  30.1 0.1 fusion.17
  30.2 0.1 reduce_window_sum.11
  30.3 0.2 select_reduce_fusion
  30.5 0.1 reduce_sum.24
  30.7 0.1 fusion.21
  30.8 0.1 copy.49
  30.8 0.1 fusion.16.placing_ref
  30.9 0.1 copy.50
  31.0 0.1 copy.51
  31.0 0.2 copy.52.prob_ref
  31.2 0.0 copy-start.5
  31.2 20.0 %recurrence.1 = f32[128,16,128]{2,1,0:T(8,128)S(1)} custom-call(f32[128,16,128]{2,1,0:T(8,128)S(1)} %bitcast.54, f32[128,16,128]{2,1,0:T(8,128)S(1)} %bitcast.55, f32[128,32]{1,0:T(8,128)S(1)} %slice.50.maps_ref, f32[16,16,128]{2,1,0:T(8,128)S(1)} %bitcast.58), custom_call_target="tpu_custom_call" | custom-call | tf_op jit(solution)/shard_map/recurrence/pallas_call | solution.py:213
  51.2 0.0 copy-start.2
  51.2 0.0 copy-start.3
  51.3 8.5 %convolution_convert_fusion.1 = bf16[128,4096]{1,0:T(8,128)(2,1)S(1)} fusion(bf16[2048,4096]{1,0:T(8,128)(2,1)} %param.25, bf16[128,2048]{1,0:T(8,128)(2,1)S(1)} %get-tuple-element.11, bf16[128,2048]{1,0:T(8,128)(2,1)S(1)} %copy-done.5, f32[16,8,16,128]{3,2,1,0:T(8,128)S(1)} %bitcast.56, f32[2048]{0:T(1024)S(1)} %copy-done.7), kind=kOutput, calls=%fused_computation.1 | convolution fusion | flops 2150629376 | bytes 19931136 | tf_op jit(solution)/shard_map/dot_general | solution.py:600
  59.8 16.8 %mixer_sum.1 = (bf16[32,4096]{1,0:T(8,128)(2,1)S(1)}, bf16[4,32,1024]{2,1,0:T(8,128)(2,1)S(1)}) custom-call(bf16[4,32,4096]{2,1,0:T(8,128)(2,1)S(1)} %bitcast.57, bf16[32,4096]{1,0:T(8,128)(2,1)S(1)} %copy-done.2, f32[1,4096]{1,0:T(1,128)S(1)} %bitcast.60), custom_call_target="tpu_custom_call" | custom-call | tf_op jit(solution)/shard_map/mixer_sum/pallas_call | solution.py:294
  76.6 35.6 %dispatch.1 = bf16[384,4096]{1,0:T(8,128)(2,1)S(1)} custom-call(bf16[384,128]{1,0:T(8,128)(2,1)S(1)} %fusion.16.placing_ref, bf16[128,1024]{1,0:T(8,128)(2,1)S(1)} %bitcast.59), custom_call_target="tpu_custom_call" | custom-call | tf_op jit(solution)/shard_map/dispatch/pallas_call | solution.py:402
  112.2 15.3 %multiply_convert_fusion.6 = bf16[384,3072]{1,0:T(8,128)(2,1)S(1)} fusion(bf16[384,4096]{1,0:T(8,128)(2,1)S(1)} %dispatch.1, bf16[4096,3072]{1,0:T(8,128)(2,1)} %param.30), kind=kOutput, calls=%fused_computation.2.clone.clone.1 | convolution fusion | flops 9669574656 | bytes 30670848 | tf_op jit(solution)/shard_map/dot_general | solution.py:540
  127.5 0.0 copy-start.1
  127.6 14.9 %convolution_convert_fusion.part_ref = bf16[384,4096]{1,0:T(8,128)(2,1)S(1)} fusion(bf16[3072,4096]{1,0:T(8,128)(2,1)} %param.31, bf16[384,3072]{1,0:T(8,128)(2,1)S(1)} %multiply_convert_fusion.6), kind=kOutput, calls=%fused_computation | convolution fusion | flops 9665249280 | bytes 30670848 | tf_op jit(solution)/shard_map/dot_general | solution.py:541
  142.5 0.1 compare_convert_fusion.pick_ref
  142.6 39.7 %bring_back.1 = bf16[32,4096]{1,0:T(8,128)(2,1)S(1)} custom-call(bf16[384,4096]{1,0:T(8,128)(2,1)S(1)} %convolution_convert_fusion.part_ref, bf16[256,384]{1,0:T(8,128)(2,1)S(1)} %compare_convert_fusion.pick_ref, f32[256,1]{1,0:T(8,128)S(1)} %copy.52.prob_ref, bf16[32,4096]{1,0:T(8,128)(2,1)S(1)} %get-tuple-element.22.mixer_ref), custom_call_target="tpu_custom_call" | custom-call | tf_op jit(solution)/shard_map/bring_back/pallas_call | solution.py:521
  182.3 0.7 copy.61
  183.0 0.7 copy.62
  (15 shorter events, 0.1 us)
Async XLA Ops:
  0.6 11.8 %copy-start = (bf16[2048,544]{0,1:T(8,128)(2,1)S(1)}, bf16[2048,544]{0,1:T(8,128)(2,1)}, u32[]{:S(2)}) copy-start(bf16[2048,544]{0,1:T(8,128)(2,1)} %param.20) | copy-start | bytes 6684676
  1.6 7.3 %collective-permute-start = (bf16[3,2048]{1,0:T(4,128)(2,1)S(1)}, bf16[3,2048]{1,0:T(4,128)(2,1)S(1)}, u32[]{:S(2)}, u32[]{:S(2)}) collective-permute-start(bf16[3,2048]{1,0:T(4,128)(2,1)S(1)} %slice.41), channel_id=1, source_target_pairs={{0,4},{4,8},{8,12},{12,16},{16,20},{20,24},{24,28},{1,5},{5,9},{9,... | collective-permute-start | bytes 36872 | tf_op jit(solution)/shard_map/ppermute | solution.py:26
  12.4 14.2 %copy-start.6 = (f32[2048]{0:T(1024)S(1)}, f32[2048]{0:T(1024)}, u32[]{:S(2)}) copy-start(f32[2048]{0:T(1024)} %param.22) | copy-start | bytes 24580
  26.6 2.9 %copy-start.4 = (f32[16,8,16,128]{3,1,2,0:T(8,128)S(1)}, f32[16,8,16,128]{3,1,2,0:T(8,128)}, u32[]{:S(2)}) copy-start(f32[16,8,16,128]{3,1,2,0:T(8,128)} %get-tuple-element.10) | copy-start | bytes 3145732
  29.5 21.7 %copy-start.7 = (f32[2048]{0:T(1024)S(1)}, f32[2048]{0:T(1024)}, u32[]{:S(2)}) copy-start(f32[2048]{0:T(1024)} %param.24) | copy-start | bytes 24580
  31.2 20.0 %copy-start.5 = (bf16[128,2048]{1,0:T(8,128)(2,1)S(1)}, bf16[128,2048]{1,0:T(8,128)(2,1)}, u32[]{:S(2)}) copy-start(bf16[128,2048]{1,0:T(8,128)(2,1)} %param.17) | copy-start | bytes 1572868
  51.2 8.6 %copy-start.2 = (bf16[32,4096]{1,0:T(8,128)(2,1)S(1)}, bf16[32,4096]{1,0:T(8,128)(2,1)}, u32[]{:S(2)}) copy-start(bf16[32,4096]{1,0:T(8,128)(2,1)} %residual_ref.1) | copy-start | bytes 786436
  51.2 8.6 %copy-start.3 = (f32[4096]{0:T(1024)S(1)}, f32[4096]{0:T(1024)}, u32[]{:S(2)}) copy-start(f32[4096]{0:T(1024)} %param.27) | copy-start | bytes 49156
  127.5 56.1 %copy-start.1 = (bf16[2048,544]{0,1:T(8,128)(2,1)S(1)}, bf16[2048,544]{0,1:T(8,128)(2,1)}, u32[]{:S(2)}) copy-start(bf16[2048,544]{0,1:T(8,128)(2,1)} %param.20) | copy-start | bytes 6684676
